TPU v7x, 32 devices: a whole 2x2x4 slice. The times are simulated.
32 devices in a mesh: groups: 2 (over y), patch: 4 (over z), sub: 4 (over x, core).
Axes of the slice: x: 2, y: 2, z: 4, core: 2. Of those that a mesh axis runs over, the one named last changes fastest.
Arguments:
- fine_nodes: float32 [32768, 128], P(('groups', 'patch', 'sub')), parts along dimension 0, may hold values from -6 to 6
- fine_edges: float32 [32768, 6, 128], P(('groups', 'patch', 'sub')), parts along dimension 0, may hold values from -6 to 6
- fine_senders: int32 [32768, 6], P(('groups', 'patch', 'sub')), parts along dimension 0, may hold values from 0 to 1279
- fine_halo: int32 [64, 128], P(('groups', 'patch', 'sub')), parts along dimension 0, may hold values from 0 to 1023
- fine_pool: int32 [32768], P(('groups', 'patch', 'sub')), parts along dimension 0, may hold values from 0 to 1023, as said below
- quarter_edges: float32 [8192, 4, 128], P(('groups', 'patch')), parts along dimension 0, may hold values from -6 to 6
- quarter_senders: int32 [8192, 4], P(('groups', 'patch')), parts along dimension 0, may hold values from 0 to 1279
- quarter_halo: int32 [16, 128], P(('groups', 'patch')), parts along dimension 0, may hold values from 0 to 1023
- quarter_pool: int32 [8192], P(('groups', 'patch')), parts along dimension 0, may hold values from 0 to 255, as said below
- coarse_edges: float32 [2048, 4, 128], P(('groups', 'patch', 'sub')), parts along dimension 0, may hold values from -6 to 6
- coarse_senders: int32 [2048, 4], P('groups'), parts along dimension 0, may hold values from 0 to 1023
- edge_in: float32 [3, 384, 128], replicated, may hold values from -0.3125 to 0.3125
- edge_out: float32 [3, 128, 128], replicated, may hold values from -0.5 to 0.5
- node_in: float32 [3, 256, 128], replicated, may hold values from -0.375 to 0.375
- node_out: float32 [3, 128, 128], replicated, may hold values from -0.5 to 0.5
Outputs:
- fine_out: float32 [32768, 128], P(('groups', 'patch', 'sub')), parts along dimension 0
There are 2 independent parts, one for each index of `groups`. A program takes and returns all parts, laid end to end along the dimension named above; an argument that names none is the same for every part. Nothing has to cross between parts.
Inputs may be any that keep to these rules, and one draw needn't show every extreme that they name: `fine_pool`: every one of a patch's 1024 quarter nodes is the target of at least one fine node of that patch. `quarter_pool`: every one of a patch's 256 sixteenth nodes is the target of at least one quarter node of that patch.
All inputs are finite; a program needn't handle non-finite values.
Results may differ from a plain program's by a relative error of at most 0.00005.
Values sent between devices are 32-bit elements; how exact they have to be, the bound alone decides.
No kernel may reach another device: no remote copies, remote signals or barrier semaphores. Data moves between devices by JAX's collectives and lax.ppermute only.
A program may use at most 128 MiB of HBM per device.

v0:
```python
import functools

import jax
import jax.numpy as jnp
from jax import lax
from jax.experimental import pallas as pl
from jax.experimental.pallas import tpu as pltpu
from jax.sharding import PartitionSpec as P


f32 = jnp.float32
half = jnp.bfloat16
LANES = 128
EPS = 1e-05


def side(x):
    high = x.astype(half)
    low = (x - high.astype(f32)).astype(half)
    return jnp.concatenate([high, low], axis=1)


def packed(w):
    row = side(w)
    return jnp.concatenate([row, row], axis=0)


def folded(y):
    w = y.shape[1] // 2
    return y[:, :w] + y[:, w:]


def times(a, b):
    return lax.dot_general(a, b, (((1,), (0,)), ((), ())), preferred_element_type=f32)


def centred_columns(w):
    return w - jnp.mean(w, axis=1, keepdims=True)


def inverse_spread(v):
    return lax.rsqrt(jnp.mean(v * v, axis=1, keepdims=True) + EPS)


def down(row):
    n = row.shape[1]
    parts = []
    for start in range(0, n, LANES):
        wide = jnp.broadcast_to(row[:, start : start + LANES], (LANES, LANES))
        parts.append(jnp.transpose(wide).astype(jnp.int16))
    return parts[0] if len(parts) == 1 else jnp.concatenate(parts, axis=0)


def picks(column, size):
    n = column.shape[0]
    lane = lax.broadcasted_iota(jnp.int32, (n, LANES), 1)
    one, zero = jnp.ones((n, LANES), half), jnp.zeros((n, LANES), half)
    parts = [
        jnp.where(column == (lane + start).astype(jnp.int16), one, zero)
        for start in range(0, size, LANES)
    ]
    return jnp.concatenate(parts, axis=1)


def members(row, size):
    n = row.shape[1]
    line = lax.broadcasted_iota(jnp.int32, (size, n), 0).astype(jnp.int16)
    entry = jnp.broadcast_to(row, (size, n)).astype(jnp.int16)
    return jnp.where(entry == line, jnp.ones((size, n), half), jnp.zeros((size, n), half))


def counts_of(pools, first, size):
    line = (lax.broadcasted_iota(jnp.int32, (size, LANES), 0) + first).astype(jnp.int16)
    one, zero = jnp.ones((size, LANES), half), jnp.zeros((size, LANES), half)
    total = zero
    for pool in pools:
        for r in range(pool.shape[0]):
            entry = jnp.broadcast_to(pool[r : r + 1, :], (size, LANES)).astype(jnp.int16)
            total = total + jnp.where(entry == line, one, zero)
    return times(total, jnp.ones((LANES, LANES), half))


def along_lanes(pool, first, lines):
    rows, n = pool.shape
    column = jnp.concatenate([down(pool[r : r + 1, :]) for r in range(rows)], axis=0)
    lane = (lax.broadcasted_iota(jnp.int32, (16, LANES), 1) + first).astype(jnp.int16)
    one, zero = jnp.ones((16, LANES), jnp.int16), jnp.zeros((16, LANES), jnp.int16)
    out = []
    for r in range(lines):
        name = lane + jnp.int16(r * LANES)
        hits = [jnp.where(column[i : i + 16, :] == name, one, zero) for i in range(0, rows * n, 16)]
        while len(hits) > 1:
            hits = [a + b for a, b in zip(hits[::2], hits[1::2])] + ([hits[-1]] if len(hits) % 2 else [])
        out.append(jnp.sum(hits[0].astype(jnp.int32).astype(f32), axis=0, keepdims=True))
    return jnp.concatenate(out, axis=0)


def first_part(degree, tile, wide, column, reach, before, extra):
    sources = wide.shape[0]
    operand = jnp.concatenate([picks(column(k), sources) for k in range(degree)], axis=0)
    sums = folded(times(operand, wide[...])).reshape(degree, tile, -1)
    for k in range(degree):
        before[k][...] = sums[k] + reach + extra[k]


def second_part(degree, tile, hidden, edge_sum, receivers, weights):
    message = folded(times(side(hidden), weights[0]))
    message = (message * inverse_spread(message)).reshape(degree, tile, -1)
    total = edge_sum
    for k in range(degree):
        total = total + message[k]
    node = jnp.concatenate([side(receivers), side(total)], axis=1)
    rhs_node = jnp.concatenate([weights[1], weights[2]], axis=0)
    node_hidden = jnp.maximum(folded(times(node, rhs_node)), 0.0)
    update = folded(times(side(node_hidden), weights[3]))
    return receivers + update * inverse_spread(update)


def pack_first(edge_in, weights):
    w = edge_in.shape[1]
    weights[0] = packed(edge_in[0:w])
    weights[1] = packed(edge_in[w : 2 * w])


def pack_second(edge_out, node_in, node_out, weights):
    w = edge_out.shape[1]
    weights[0] = packed(centred_columns(edge_out[...]))
    weights[1] = packed(node_in[0:w])
    weights[2] = packed(node_in[w : 2 * w])
    weights[3] = packed(centred_columns(node_out[...]))


def with_halo(degree, tile, rows, margin, beyond, column, before):
    chosen = [picks(column(k) - jnp.int16(rows), 2 * margin) for k in range(degree)]
    sums = folded(times(jnp.concatenate(chosen, axis=0), beyond[...])).reshape(degree, tile, -1)
    parts = [jnp.maximum(sums[k] + before[k][...], 0.0) for k in range(degree)]
    return jnp.concatenate(parts, axis=0)


def halo_sources(left, right, sender, beyond):
    margin = left.shape[0]
    beyond[:margin, :] = side(folded(times(side(left[...]), sender)))
    beyond[margin:, :] = side(folded(times(side(right[...]), sender)))


def rotated(target, flip, part):
    return jnp.where(target < part, target + flip * part, target - flip * part)


def gather_halo(lists, nodes, to_next, to_previous):
    both = side(nodes[...])
    for i, out in enumerate((to_next, to_previous)):
        out[...] = folded(times(picks(down(lists[i : i + 1, :]), nodes.shape[0]), both))


def start_kernel(lists, nodes, senders, pool, edge_in, edges, to_next, to_previous, kept_nodes, kept_senders, kept_pool, weights, *refs):
    slots, (kept_lists, kept_layer, arrived) = refs[:-3], refs[-3:]
    moves = [(lists, kept_lists), (nodes, kept_nodes), (edge_in.at[0], kept_layer), (senders, kept_senders), (pool, kept_pool)]
    moves += [(edges.at[k], slots[k]) for k in range(len(slots))]
    copies = [pltpu.make_async_copy(*move, arrived.at[i]) for i, move in enumerate(moves)]
    for copy in copies:
        copy.start()
    copies[0].wait()
    copies[1].wait()
    gather_halo(kept_lists, kept_nodes, to_next, to_previous)
    copies[2].wait()
    pack_first(kept_layer, weights)
    w = nodes.shape[1]
    weights[2] = packed(kept_layer[2 * w : 3 * w])
    for copy in copies[3:]:
        copy.wait()


def fine_first_kernel(ready, lines, flip, senders, nodes, pool, weights, edges, *refs):
    degree = edges.shape[0]
    here, refs = refs[:ready], refs[ready:]
    before, refs = refs[:degree], refs[degree:]
    edge_sum, counts, wide, local, arrived = refs
    rows, _ = nodes.shape
    copies = [pltpu.make_async_copy(edges.at[k], local.at[k - ready], arrived.at[k - ready]) for k in range(ready, degree)]
    for copy in copies:
        copy.start()
    wide[:rows, :] = side(folded(times(side(nodes[...]), weights[0])))
    wide[rows:, :] = weights[2]
    reach = folded(times(side(nodes[...]), weights[1]))
    part = lines * LANES
    height = counts.shape[0] // 2
    counts[...] = jnp.zeros_like(counts)
    counts[:lines, :] = along_lanes(pool, flip[0] * part, lines)
    counts[height : height + lines, :] = along_lanes(pool, (1 - flip[0]) * part, lines)
    for k in range(degree):
        if k == ready:
            for copy in copies:
                copy.wait()
        column = down(senders[k : k + 1, :])
        edge = here[k][...] if k < ready else local[k - ready]
        operand = jnp.concatenate([picks(column, rows), side(edge)], axis=1)
        before[k][...] = folded(times(operand, wide[...])) + reach
        edge_sum[...] = edge if k == 0 else edge_sum[...] + edge


def fine_second_kernel(flip, senders, pool, nodes, left, right, counts, *refs):
    degree = senders.shape[0]
    before, refs = refs[:degree], refs[degree:]
    edge_sum, edge_in, edge_out, node_in, node_out, new, keep, send, beyond, weights, held, sent = refs
    rows, w = nodes.shape
    margin = left.shape[0]
    halo_sources(left, right, packed(edge_in[0, 0:w]), beyond)
    pack_second(edge_out.at[0], node_in.at[0], node_out.at[0], weights)
    hidden = with_halo(degree, rows, rows, margin, beyond, lambda k: down(senders[k : k + 1, :]), before)
    held[...] = second_part(degree, rows, hidden, edge_sum[...], nodes[...], weights)
    copy = pltpu.make_async_copy(held, new, sent)
    copy.start()
    both = side(held[...])
    height = counts.shape[0] // 2
    part = keep.shape[0] - height
    target = jnp.concatenate([pool[j : j + 1, :] for j in range(pool.shape[0])], axis=1)
    target = rotated(target, flip[0], part)
    send[:part, :] = folded(times(members(target - part, part), both))
    keep[:part, :] = folded(times(members(target, part), both))
    keep[part:, :] = counts[:height, :]
    send[part:, :] = counts[height:, :]
    copy.wait()


def window_kernel(
    flip, quarter_pool, fine_pool, quarter_edges, coarse_senders, edge_in, edge_out, node_in, node_out, _,
    coarse_share, chosen, quarter_before, quarter_sum, coarse_columns,
    quarter_first, quarter_second, coarse_first, coarse_second,
):
    w = edge_in.shape[2]
    block = coarse_share.shape[0]
    share = 1.0 / counts_of([quarter_pool[...]], 0, block)
    coarse_share[...] = share

    degree, rows, _ = quarter_before.shape
    rhs = packed(edge_in[1, 2 * w : 3 * w])
    total = None
    for k in range(degree):
        edge = quarter_edges[pl.ds(k, rows, stride=degree), :]
        total = edge if total is None else total + edge
        quarter_before[k] = folded(times(side(edge), rhs))
    quarter_sum[...] = total
    pack_first(edge_in.at[1], quarter_first)
    pack_second(edge_out.at[1], node_in.at[1], node_out.at[1], quarter_second)
    pack_first(edge_in.at[2], coarse_first)
    coarse_first[2] = packed(edge_in[2, 2 * w : 3 * w])
    pack_second(edge_out.at[2], node_in.at[2], node_out.at[2], coarse_second)

    for k in range(coarse_columns.shape[0]):
        for start in range(0, block, LANES):
            coarse_columns[k, start : start + LANES, :] = down(coarse_senders[k : k + 1, start : start + LANES])

    parent = [down(quarter_pool[r : r + 1, :]) for r in range(quarter_pool.shape[0])]
    parent = side(jnp.concatenate(parent, axis=0).astype(jnp.int32).astype(f32))
    for r in range(fine_pool.shape[0]):
        rows = slice(r * LANES, (r + 1) * LANES)
        column = down(fine_pool[r : r + 1, :])
        named = folded(times(picks(column, parent.shape[0]), parent))
        chosen[rows, :] = picks(named.astype(jnp.int32).astype(jnp.int16), chosen.shape[1])


def mean_kernel(lines, mine, theirs, out):
    part = out.shape[0]
    counts = mine[part : part + lines, :] + theirs[part : part + lines, :]
    for r in range(lines):
        rows = slice(r * LANES, (r + 1) * LANES)
        share = 1.0 / jnp.transpose(jnp.broadcast_to(counts[r : r + 1, :], (LANES, LANES)))
        out[rows, :] = (mine[rows, :] + theirs[rows, :]) * share


def quarter_nodes_kernel(flip, mine, other, lists, nodes, to_next, to_previous):
    part = mine.shape[0]
    nodes[pl.ds(pl.multiple_of(flip[0] * part, part), part), :] = mine[...]
    nodes[pl.ds(pl.multiple_of((1 - flip[0]) * part, part), part), :] = other[...]
    gather_halo(lists, nodes, to_next, to_previous)


def quarter_first_kernel(tile, senders, nodes, extra, weights, before, wide):
    degree, rows, _ = before.shape
    wide[...] = side(folded(times(side(nodes[...]), weights[0])))
    for t in range(rows // tile):
        span = slice(t * tile, (t + 1) * tile)
        reach = folded(times(side(nodes[span, :]), weights[1]))
        first_part(
            degree, tile, wide, lambda k: down(senders[k : k + 1, span]), reach,
            [before.at[k, span, :] for k in range(degree)], extra.at[:, span, :],
        )


def quarter_second_kernel(
    flip, senders, pool, nodes, left, right, before, edge_sum, share, first_weights, weights, new, own, partner, beyond,
):
    degree, rows, _ = before.shape
    margin = left.shape[0]
    halo_sources(left, right, first_weights[0], beyond)
    hidden = with_halo(
        degree, rows, rows, margin, beyond, lambda k: down(senders[k : k + 1, :]),
        [before.at[k] for k in range(degree)],
    )
    updated = second_part(degree, rows, hidden, edge_sum[...], nodes[...], weights)
    new[...] = updated
    part = own.shape[0]
    target = jnp.concatenate([pool[j : j + 1, :] for j in range(pool.shape[0])], axis=1)
    target = rotated(target, flip[0], part)
    split = side(updated)
    first = pl.multiple_of(flip[0] * part, part)
    second = pl.multiple_of((1 - flip[0]) * part, part)
    own[...] = folded(times(members(target, part), split)) * share[pl.ds(first, part), :]
    partner[...] = folded(times(members(target - part, part), split)) * share[pl.ds(second, part), :]


def base_kernel(pool, quarter, fine_new, out):
    both = side(quarter[...])
    column = jnp.concatenate([down(pool[r : r + 1, :]) for r in range(pool.shape[0])], axis=0)
    out[...] = fine_new[...] + folded(times(picks(column, both.shape[0]), both))


def coarse_kernel(n_patch, tile, place, *refs):
    mine, refs = refs[:n_patch], refs[n_patch:]
    other, refs = refs[:n_patch], refs[n_patch:]
    (columns, chosen, base, first_weights, weights), refs = refs[:5], refs[5:]
    pieces, (out, nodes, edges, wide, new, held, sent) = refs[:-7], refs[-7:]
    part, w = mine[0].shape
    block = 2 * part
    piece = pieces[0].shape[0]
    degree = columns.shape[0]
    sources = nodes.shape[0]
    for j, source in enumerate(pieces):
        at = jnp.bitwise_xor(place[2], j)
        edges[pl.ds(pl.multiple_of(at * piece, piece), piece), :] = source[...]
    for j in range(n_patch):
        at = lax.rem(place[0] + j, n_patch) * block
        nodes[pl.ds(pl.multiple_of(at + place[1] * part, part), part), :] = mine[j][...]
        nodes[pl.ds(pl.multiple_of(at + (1 - place[1]) * part, part), part), :] = other[j][...]
    wide[:sources, :] = side(folded(times(side(nodes[...]), first_weights[0])))
    wide[sources:, :] = first_weights[2]
    for t in range(block // tile):
        span = slice(t * tile, (t + 1) * tile)
        receivers = nodes[pl.ds(pl.multiple_of(place[0] * block + t * tile, tile), tile), :]
        reach = folded(times(side(receivers), first_weights[1]))
        edge = [edges[pl.ds(t * tile * degree + k, tile, stride=degree), :] for k in range(degree)]
        operand = [jnp.concatenate([picks(columns[k, span, :], sources), side(edge[k])], axis=1) for k in range(degree)]
        sums = folded(times(jnp.concatenate(operand, axis=0), wide[...])).reshape(degree, tile, w)
        hidden = jnp.maximum(sums + reach[None], 0.0).reshape(degree * tile, w)
        total = edge[0]
        for k in range(1, degree):
            total = total + edge[k]
        new[span, :] = second_part(degree, tile, hidden, total, receivers, weights)
    both = side(new[...])
    steps = sent.shape[0]
    rows = out.shape[0] // steps
    copies = []
    for i in range(steps):
        span = slice(i * rows, (i + 1) * rows)
        held[span, :] = base[span, :] + folded(times(chosen[span, :], both))
        copies.append(pltpu.make_async_copy(held.at[span, :], out.at[span, :], sent.at[i]))
        copies[-1].start()
    for copy in copies:
        copy.wait()


def whole(*shape):
    return pl.BlockSpec(shape, lambda *_: (0,) * len(shape))


def shaped(*shape, dtype=f32):
    return jax.ShapeDtypeStruct(shape, dtype)


def run(kernel, grid, scalars, in_specs, operands, outs, out_specs, scratch, mega, flops):
    return pl.pallas_call(
        kernel,
        out_shape=outs,
        grid_spec=pltpu.PrefetchScalarGridSpec(
            num_scalar_prefetch=len(scalars), grid=grid, in_specs=in_specs, out_specs=out_specs,
            scratch_shapes=scratch,
        ),
        compiler_params=pltpu.CompilerParams(vmem_limit_bytes=mega * 1024 * 1024),
        cost_estimate=pl.CostEstimate(flops=flops, bytes_accessed=10**6, transcendentals=0),
    )(*scalars, *operands)


def passed(value, axis, steps):
    count = lax.axis_size(axis)
    return lax.ppermute(value, axis, [(s, (s + steps) % count) for s in range(count)])


def swapped(value, axis, bit):
    count = lax.axis_size(axis)
    return lax.ppermute(value, axis, [(s, s ^ bit) for s in range(count)])


def on_device(
    fine_nodes, fine_edges, fine_senders, fine_halo, fine_pool, quarter_edges, quarter_senders,
    quarter_halo, quarter_pool, coarse_edges, coarse_senders, edge_in, edge_out, node_in, node_out,
):
    n_sub, n_patch = lax.axis_size("sub"), lax.axis_size("patch")
    sub, patch = lax.axis_index("sub").astype(jnp.int32), lax.axis_index("patch").astype(jnp.int32)
    rows, degree, w = fine_edges.shape
    q_rows, q_degree, _ = quarter_edges.shape
    margin, q_margin = fine_halo.shape[1], quarter_halo.shape[1]
    piece, c_degree, _ = coarse_edges.shape
    total = coarse_senders.shape[0]
    block = total // n_patch
    part, c_part = q_rows // 2, block // 2
    tile = min(512, q_rows)
    c_tile = min(256, block)
    lines = part // LANES
    height = -(-lines // 8) * 8
    core = sub % 2
    flip = core.reshape(1)
    patch_core = jnp.stack([patch, core])
    layers = (edge_in, edge_out, node_in, node_out)
    layer_specs = [whole(*x.shape) for x in layers]
    in_hbm, in_vmem = pl.BlockSpec(memory_space=pl.ANY), pl.BlockSpec(memory_space=pltpu.VMEM)
    pool_rows = fine_pool.reshape(rows // LANES, LANES)
    quarter_pool_rows = quarter_pool.reshape(q_rows // LANES, LANES)
    fine_senders, quarter_senders, coarse_senders = fine_senders.T, quarter_senders.T, coarse_senders.T
    own_edges = coarse_edges.reshape(piece * c_degree, w)
    hbm = lambda x: pltpu.with_memory_space_constraint(x, pltpu.HBM)
    mats = lambda n: (n, 2 * w, 2 * w)
    short = jnp.int16
    big = 16 if total <= 2048 else 48

    ready = min(2, degree - 1)
    edges = hbm(fine_edges.transpose(1, 0, 2))
    to_next, to_previous, nodes, senders, pool, fine_weights, *here = run(
        start_kernel, (1,), (), [in_hbm] * 6,
        (hbm(fine_halo), hbm(fine_nodes), hbm(fine_senders), hbm(pool_rows), hbm(edge_in), edges),
        (
            shaped(margin, w), shaped(margin, w), shaped(rows, w), shaped(degree, rows, dtype=jnp.int32),
            shaped(*pool_rows.shape, dtype=jnp.int32), shaped(*mats(3), dtype=half), *(shaped(rows, w),) * ready,
        ),
        [
            whole(margin, w), whole(margin, w), in_vmem, in_vmem, in_vmem, whole(*mats(3)), *[in_vmem] * ready,
        ],
        [pltpu.VMEM((2, margin), jnp.int32), pltpu.VMEM((3 * w, w), f32), pltpu.SemaphoreType.DMA((ready + 5,))],
        8, 10**8,
    )
    left = passed(to_next, ("patch", "sub"), 1)
    right = passed(to_previous, ("patch", "sub"), -1)
    firsts = run(
        functools.partial(fine_first_kernel, ready, lines), (1,), (flip,),
        [whole(degree, rows), whole(rows, w), whole(*pool_rows.shape), whole(*mats(3)), in_hbm, *[whole(rows, w)] * ready],
        (senders, nodes, pool, fine_weights, edges, *here),
        (*(shaped(rows, w),) * (degree + 1), shaped(2 * height, w)),
        [whole(rows, w)] * (degree + 1) + [whole(2 * height, w)],
        [
            pltpu.VMEM((rows + 2 * w, 2 * w), half),
            pltpu.VMEM((degree - ready, rows, w), f32), pltpu.SemaphoreType.DMA((degree - ready,)),
        ],
        30, 8 * 10**9,
    )
    *before, edge_sum, counts = firsts
    fine_new, keep, send = run(
        fine_second_kernel, (1,), (flip,),
        [
            whole(degree, rows), whole(*pool_rows.shape), whole(rows, w), whole(margin, w), whole(margin, w),
            whole(2 * height, w), *[whole(rows, w)] * (degree + 1), *layer_specs,
        ],
        (fine_senders, pool_rows, fine_nodes, left, right, counts, *before, edge_sum, *layers),
        (pltpu.HBM((rows, w), f32), shaped(part + height, w), shaped(part + height, w)),
        [in_hbm, whole(part + height, w), whole(part + height, w)],
        [
            pltpu.VMEM((2 * margin, 2 * w), half), pltpu.VMEM(mats(4), half), pltpu.VMEM((rows, w), f32),
            pltpu.SemaphoreType.DMA,
        ],
        30, 4 * 10**9,
    )

    mine, theirs = keep, swapped(send, "sub", 1)
    bit = 2
    after = theirs
    while bit < n_sub:
        mine = mine + theirs
        theirs = swapped(mine, "sub", bit)
        after = mine if bit == 2 else after
        bit *= 2
    (coarse_share, chosen, quarter_before, quarter_sum, coarse_columns,
     quarter_weights, quarter_later, coarse_weights, coarse_later) = run(
        window_kernel, (1,), (patch_core,),
        [
            whole(*quarter_pool_rows.shape), whole(*pool_rows.shape),
            whole(q_rows * q_degree, w),
            pl.BlockSpec((c_degree, block), lambda i, place: (0, place[0])), *layer_specs, in_hbm,
        ],
        (quarter_pool_rows, pool_rows, quarter_edges.reshape(q_rows * q_degree, w), coarse_senders,
         *layers, after),
        (
            shaped(block, w), shaped(rows, block, dtype=half), shaped(q_degree, q_rows, w), shaped(q_rows, w),
            shaped(c_degree, block, w, dtype=short), shaped(*mats(2), dtype=half), shaped(*mats(4), dtype=half),
            shaped(*mats(3), dtype=half), shaped(*mats(4), dtype=half),
        ),
        [
            whole(block, w), whole(rows, block), whole(q_degree, q_rows, w), whole(q_rows, w),
            whole(c_degree, block, w), whole(*mats(2)), whole(*mats(4)), whole(*mats(3)),
            whole(*mats(4)),
        ],
        [], 16, 10**9,
    )
    mine = run(
        functools.partial(mean_kernel, lines), (1,), (), [whole(part + height, w)] * 2, (mine, theirs),
        shaped(part, w), whole(part, w), [], 6, 10**7,
    )
    other = swapped(mine, "sub", 1)

    quarter_nodes, to_next, to_previous = run(
        quarter_nodes_kernel, (1,), (flip,), [whole(part, w), whole(part, w), whole(2, q_margin)],
        (mine, other, quarter_halo), (shaped(q_rows, w), shaped(q_margin, w), shaped(q_margin, w)),
        [whole(q_rows, w), whole(q_margin, w), whole(q_margin, w)], [], 8, 10**8,
    )
    left = passed(to_next, "patch", 1)
    right = passed(to_previous, "patch", -1)
    across = [own_edges]
    bit = 2
    while bit < n_sub:
        across += [swapped(value, "sub", bit) for value in across]
        bit *= 2
    edge_pieces = []
    for value in across:
        edge_pieces += [value, swapped(value, "sub", 1)]
    quarter_first = run(
        functools.partial(quarter_first_kernel, tile), (1,), (),
        [whole(q_degree, q_rows), whole(q_rows, w), whole(q_degree, q_rows, w), whole(*mats(2))],
        (quarter_senders, quarter_nodes, quarter_before, quarter_weights),
        shaped(q_degree, q_rows, w), whole(q_degree, q_rows, w), [pltpu.VMEM((q_rows, 2 * w), half)], 20, 3 * 10**9,
    )
    quarter_new, own, own_partner = run(
        quarter_second_kernel, (1,), (flip,),
        [
            whole(q_degree, q_rows), whole(*quarter_pool_rows.shape), whole(q_rows, w), whole(q_margin, w),
            whole(q_margin, w), whole(q_degree, q_rows, w), whole(q_rows, w), whole(block, w), whole(*mats(2)),
            whole(*mats(4)),
        ],
        (quarter_senders, quarter_pool_rows, quarter_nodes, left, right, quarter_first, quarter_sum, coarse_share,
         quarter_weights, quarter_later),
        (shaped(q_rows, w), shaped(c_part, w), shaped(c_part, w)),
        [whole(q_rows, w), whole(c_part, w), whole(c_part, w)],
        [pltpu.VMEM((2 * q_margin, 2 * w), half)], 20, 2 * 10**9,
    )

    pieces = [own] + [passed(own, "patch", -j) for j in range(1, n_patch)]
    partner = [own_partner] + [swapped(pieces[j], "sub", 1) for j in range(1, n_patch)]
    base = run(
        base_kernel, (1,), (), [whole(*pool_rows.shape), whole(q_rows, w), whole(rows, w)],
        (pool_rows, quarter_new, hbm(fine_new)), shaped(rows, w), whole(rows, w), [], 16, 10**9,
    )
    return run(
        functools.partial(coarse_kernel, n_patch, c_tile), (1,), (jnp.stack([patch, core, sub]),),
        [
            *[whole(c_part, w)] * (2 * n_patch), whole(c_degree, block, w), whole(rows, block), whole(rows, w),
            whole(*mats(3)), whole(*mats(4)), *[whole(*own_edges.shape)] * n_sub,
        ],
        (*pieces, *partner, coarse_columns, chosen, base, coarse_weights, coarse_later, *edge_pieces),
        shaped(rows, w), in_hbm,
        [
            pltpu.VMEM((total, w), f32), pltpu.VMEM((block * c_degree, w), f32),
            pltpu.VMEM((total + 2 * w, 2 * w), half), pltpu.VMEM((block, w), f32), pltpu.VMEM((rows, w), f32),
            pltpu.SemaphoreType.DMA((4,)),
        ],
        big, 2 * 10**9,
    )


def solution(mesh):
    split = P(("groups", "patch", "sub"))
    patches = P(("groups", "patch"))
    return jax.shard_map(
        on_device,
        mesh=mesh,
        in_specs=(
            split, split, split, split, split, patches, patches, patches, patches, split, P("groups"),
            P(), P(), P(), P(),
        ),
        out_specs=split,
        check_vma=False,
    )
```

profile of v0, /device:TPU:0, one launch (start us, length us, event | category | flops | bytes accessed | tf_op | source)
XLA Modules:
  0.0 63.8 jit_solution(15073277096595710671)
XLA Ops:
  0.0 1.5 %shard_map.145 = (f32[128,128]{1,0:T(8,128)S(1)}, f32[128,128]{1,0:T(8,128)S(1)}, f32[1024,128]{1,0:T(8,128)S(1)}, s32[6,1024]{1,0:T(8,128)S(1)}, s32[8,128]{1,0...) custom-call(s32[2,128]{1,0:T(2,128)} %lists.2, ...), custom_call_target="tpu_custom_call" | custom-call | flops 100000000 | bytes 1000000 | tf_op jit(solution)/shard_map/pallas_call | solution.py:372
  1.5 0.5 collective-permute-start
  2.1 5.0 %collective-permute-start.1 = (f32[128,128]{1,0:T(8,128)S(1)}, f32[128,128]{1,0:T(8,128)S(1)}, u32[]{:S(2)}, u32[]{:S(2)}) collective-permute-start(f32[128,128]{1,0:T(8,128)S(1)} %get-tuple-element.40), channel_id=1, source_target_pairs={{0,15},{1,0},{2,1},{3,2},{4,3},{5,4},{6,5},{7,6},{8,7},{9,8},{10,9... | collective-permute-start | bytes 196616 | tf_op jit(solution)/shard_map/ppermute | solution.py:386
  7.1 5.7 %shard_map.146 = (f32[1024,128]{1,0:T(8,128)S(1)}, f32[1024,128]{1,0:T(8,128)S(1)}, f32[1024,128]{1,0:T(8,128)S(1)}, f32[1024,128]{1,0:T(8,128)S(1)}, f32[1024,1...) custom-call(s32[1]{0:T(128)} %bitcast.1.flip, ...), custom_call_target="tpu_custom_call" | custom-call | flops 8000000000 | bytes 1000000 | tf_op jit(solution)/shard_map/pallas_call | solution.py:372
  13.0 3.6 %shard_map.147 = (f32[1024,128]{1,0:T(8,128)}, f32[520,128]{1,0:T(8,128)S(1)}, f32[520,128]{1,0:T(8,128)S(1)}) custom-call(s32[1]{0:T(128)} %bitcast.1.flip, s32[6,1024]{1,0:T(8,128)S(1)} %bitcast.13, s32[8,128]{1,0:T(8,128)S(1)} %bitcast.16, f32[1024,128]{1,0:T(8,128)S(1)} %copy-done.2, f32[128,128]{1,0:T(8,128)S(1)} %collective-permute-done.left, ...), custom_call_target="tpu_custom_call" | custom-call | flops 4000000000 | bytes 1000000 | tf_op jit(solution)/shard_map/pallas_call | solution.py:372
  16.7 1.5 %collective-permute-done.2 = f32[520,128]{1,0:T(8,128)S(1)} collective-permute-done((f32[520,128]{1,0:T(8,128)S(1)}, f32[520,128]{1,0:T(8,128)S(1)}, u32[]{:S(2)}, u32[]{:S(2)}) %collective-permute-start.2) | collective-permute-done | bytes 266272 | tf_op jit(solution)/shard_map/ppermute | solution.py:391
  18.4 8.4 %collective-permute-done.3.theirs = f32[520,128]{1,0:T(8,128)S(1)} collective-permute-done((f32[520,128]{1,0:T(8,128)S(1)}, f32[520,128]{1,0:T(8,128)S(1)}, u32[]{:S(2)}, u32[]{:S(2)}) %collective-permute-start.3) | collective-permute-done | bytes 266272 | tf_op jit(solution)/shard_map/ppermute | solution.py:391
  27.0 0.4 collective-permute-start.14
  27.6 5.6 %collective-permute-done.14.refs_15_ = f32[256,128]{1,0:T(8,128)} collective-permute-done((f32[256,128]{1,0:T(8,128)}, f32[256,128]{1,0:T(8,128)}, u32[]{:S(2)}, u32[]{:S(2)}) %collective-permute-start.14) | collective-permute-done | bytes 131104 | tf_op jit(solution)/shard_map/ppermute | solution.py:391
  33.2 1.0 %copy-done.4 = f32[3,256,128]{2,1,0:T(8,128)S(1)} copy-done((f32[3,256,128]{2,1,0:T(8,128)S(1)}, f32[3,256,128]{2,1,0:T(8,128)}, u32[]{:S(2)}) %copy-start.4) | copy-done | bytes 393240
  34.2 0.9 %copy-done.6 = f32[3,128,128]{2,1,0:T(8,128)S(1)} copy-done((f32[3,128,128]{2,1,0:T(8,128)S(1)}, f32[3,128,128]{2,1,0:T(8,128)}, u32[]{:S(2)}) %copy-start.6) | copy-done | bytes 196632
  35.2 0.9 %copy-done.8 = f32[3,128,128]{2,1,0:T(8,128)S(1)} copy-done((f32[3,128,128]{2,1,0:T(8,128)S(1)}, f32[3,128,128]{2,1,0:T(8,128)}, u32[]{:S(2)}) %copy-start.8) | copy-done | bytes 196632
  36.1 1.9 %shard_map.150 = (f32[256,128]{1,0:T(8,128)S(1)}, bf16[1024,256]{1,0:T(8,128)(2,1)S(1)}, f32[4,1024,128]{2,1,0:T(8,128)S(1)}, f32[1024,128]{1,0:T(8,128)S(1)}, s...) custom-call(s32[2]{0:T(128)S(1)} %pad_add_fusion.1.flip, ...), custom_call_target="tpu_custom_call" | custom-call | flops 1000000000 | bytes 1000000 | tf_op jit(solution)/shard_map/pallas_call | solution.py:372
  38.0 0.4 shard_map.149
  38.6 3.6 %collective-permute-start.6 = (f32[128,128]{1,0:T(8,128)S(1)}, f32[128,128]{1,0:T(8,128)S(1)}, u32[]{:S(2)}, u32[]{:S(2)}) collective-permute-start(f32[128,128]{1,0:T(8,128)S(1)} %get-tuple-element.59), channel_id=1, source_target_pairs={{0,12},{4,0},{8,4},{12,8},{1,13},{5,1},{9,5},{13,9},{2,14},{6,2},{... | collective-permute-start | bytes 196616 | tf_op jit(solution)/shard_map/ppermute | solution.py:386
  42.3 2.6 %shard_map.151.before = f32[4,1024,128]{2,1,0:T(8,128)S(1)} custom-call(s32[4,1024]{1,0:T(4,128)S(1)} %bitcast.21, f32[1024,128]{1,0:T(8,128)S(1)} %get-tuple-element.57.nodes, f32[4,1024,128]{2,1,0:T(8,128)S(1)} %get-tuple-element.60.extra, bf16[2,256,256]{2,1,0:T(8,128)(2,1)S(1)} %get-tuple-element.61.weights.first_weights), custom_call_target="tpu_custom_call" | custom-call | flops 3000000000 | bytes 1000000 | tf_op jit(solution)/shard_map/pallas_call | solution.py:372
  45.2 2.6 %shard_map.152 = (f32[1024,128]{1,0:T(8,128)S(1)}, f32[128,128]{1,0:T(8,128)S(1)}, f32[128,128]{1,0:T(8,128)S(1)}) custom-call(s32[1]{0:T(128)} %bitcast.1.flip, s32[4,1024]{1,0:T(4,128)S(1)} %bitcast.22, s32[8,128]{1,0:T(8,128)S(1)} %bitcast.20, f32[1024,128]{1,0:T(8,128)S(1)} %get-tuple-element.57.nodes, f32[128,128]{1,0:T(8,128)S(1)} %collective-permute-done.5.left, ...), custom_call_target="tpu_custom_call" | custom-call | flops 2000000000 | bytes 1000000 | tf_op jit(solution)/shard_map/pallas_call | solution.py:372
  47.8 3.2 %collective-permute-start.7 = (f32[128,128]{1,0:T(8,128)S(1)}, f32[128,128]{1,0:T(8,128)S(1)}, u32[]{:S(2)}, u32[]{:S(2)}) collective-permute-start(f32[128,128]{1,0:T(8,128)S(1)} %get-tuple-element.65.refs_0_), channel_id=1, source_target_pairs={{0,12},{4,0},{8,4},{12,8},{1,13},{5,1},{9,5},{13,9},{2,14},{6,2},{... | collective-permute-start | bytes 196616 | tf_op jit(solution)/shard_map/ppermute | solution.py:386
  51.0 0.6 %collective-permute-start.9 = (f32[128,128]{1,0:T(8,128)S(1)}, f32[128,128]{1,0:T(8,128)S(1)}, u32[]{:S(2)}, u32[]{:S(2)}) collective-permute-start(f32[128,128]{1,0:T(8,128)S(1)} %get-tuple-element.65.refs_0_), channel_id=1, source_target_pairs={{0,4},{4,8},{8,12},{12,0},{1,5},{5,9},{9,13},{13,1},{2,6},{6,10},{... | collective-permute-start | bytes 196616 | tf_op jit(solution)/shard_map/ppermute | solution.py:386
  51.7 1.3 %collective-permute-done.7.refs_1_ = f32[128,128]{1,0:T(8,128)S(1)} collective-permute-done((f32[128,128]{1,0:T(8,128)S(1)}, f32[128,128]{1,0:T(8,128)S(1)}, u32[]{:S(2)}, u32[]{:S(2)}) %collective-permute-start.7) | collective-permute-done | bytes 65568 | tf_op jit(solution)/shard_map/ppermute | solution.py:386
  52.9 3.2 %collective-permute-done.8.refs_2_ = f32[128,128]{1,0:T(8,128)S(1)} collective-permute-done((f32[128,128]{1,0:T(8,128)S(1)}, f32[128,128]{1,0:T(8,128)S(1)}, u32[]{:S(2)}, u32[]{:S(2)}) %collective-permute-start.8) | collective-permute-done | bytes 65568 | tf_op jit(solution)/shard_map/ppermute | solution.py:386
  56.1 0.9 %collective-permute-done.9.refs_3_ = f32[128,128]{1,0:T(8,128)S(1)} collective-permute-done((f32[128,128]{1,0:T(8,128)S(1)}, f32[128,128]{1,0:T(8,128)S(1)}, u32[]{:S(2)}, u32[]{:S(2)}) %collective-permute-start.9) | collective-permute-done | bytes 65568 | tf_op jit(solution)/shard_map/ppermute | solution.py:386
  57.0 1.8 %shard_map.153.refs_10_ = f32[1024,128]{1,0:T(8,128)S(1)} custom-call(s32[8,128]{1,0:T(8,128)S(1)} %bitcast.18, f32[1024,128]{1,0:T(8,128)S(1)} %get-tuple-element.69.quarter, f32[1024,128]{1,0:T(8,128)} %get-tuple-element.70.fine_new), custom_call_target="tpu_custom_call" | custom-call | flops 1000000000 | bytes 1000000 | tf_op jit(solution)/shard_map/pallas_call | solution.py:372
  58.9 4.7 %shard_map.154 = f32[1024,128]{1,0:T(8,128)} custom-call(s32[3]{0:T(128)S(1)} %pad_add_fusion.place, f32[128,128]{1,0:T(8,128)S(1)} %get-tuple-element.65.refs_0_, f32[128,128]{1,0:T(8,128)S(1)} %collective-permute-done.7.refs_1_, f32[128,128]{1,0:T(8,128)S(1)} %collective-permute-done.8.refs_2_, f32[128,128]{1,0:T(8,128)S(1)} %collective-permute-done.9.refs_3_, ...), custom_call_target="tpu_custom_call" | custom-call | flops 2000000000 | bytes 1000000 | tf_op jit(solution)/shard_map/pallas_call | solution.py:372
  (51 shorter events, 1.4 us)
Async XLA Ops:
  1.5 11.3 %collective-permute-start = (f32[128,128]{1,0:T(8,128)S(1)}, f32[128,128]{1,0:T(8,128)S(1)}, u32[]{:S(2)}, u32[]{:S(2)}) collective-permute-start(f32[128,128]{1,0:T(8,128)S(1)} %get-tuple-element.39), channel_id=1, source_target_pairs={{0,1},{1,2},{2,3},{3,4},{4,5},{5,6},{6,7},{7,8},{8,9},{9,10},{10,1... | collective-permute-start | bytes 196616 | tf_op jit(solution)/shard_map/ppermute | solution.py:386
  2.1 10.8 %collective-permute-start.1 = (f32[128,128]{1,0:T(8,128)S(1)}, f32[128,128]{1,0:T(8,128)S(1)}, u32[]{:S(2)}, u32[]{:S(2)}) collective-permute-start(f32[128,128]{1,0:T(8,128)S(1)} %get-tuple-element.40), channel_id=1, source_target_pairs={{0,15},{1,0},{2,1},{3,2},{4,3},{5,4},{6,5},{7,6},{8,7},{9,8},{10,9... | collective-permute-start | bytes 196616 | tf_op jit(solution)/shard_map/ppermute | solution.py:386
  7.1 5.8 %copy-start.7 = (f32[3,128,128]{2,1,0:T(8,128)S(1)}, f32[3,128,128]{2,1,0:T(8,128)}, u32[]{:S(2)}) copy-start(f32[3,128,128]{2,1,0:T(8,128)} %node_out.1) | copy-start | bytes 589828
  7.1 5.8 %copy-start.9 = (s32[1024,6]{0,1:T(8,128)S(1)}, s32[1024,6]{0,1:T(8,128)}, u32[]{:S(2)}) copy-start(s32[1024,6]{0,1:T(8,128)} %param.17) | copy-start | bytes 73732
  7.1 5.8 %copy-start.11 = (s32[1024]{0:T(1024)S(1)}, s32[1024]{0:T(1024)}, u32[]{:S(2)}) copy-start(s32[1024]{0:T(1024)} %param.19) | copy-start | bytes 12292
  13.0 20.3 %copy-start.1 = (f32[1024,4,128]{2,1,0:T(4,128)S(1)}, f32[1024,4,128]{2,1,0:T(4,128)}, u32[]{:S(2)}) copy-start(f32[1024,4,128]{2,1,0:T(4,128)} %param.20) | copy-start | bytes 6291460
  13.0 20.3 %copy-start.10 = (s32[1024,4]{0,1:T(4,128)S(1)}, s32[1024,4]{0,1:T(4,128)}, u32[]{:S(2)}) copy-start(s32[1024,4]{0,1:T(4,128)} %param.25) | copy-start | bytes 49156
  13.0 20.2 %copy-start.12 = (s32[1024]{0:T(1024)S(1)}, s32[1024]{0:T(1024)}, u32[]{:S(2)}) copy-start(s32[1024]{0:T(1024)} %param.23) | copy-start | bytes 12292
  16.6 1.6 %collective-permute-start.2 = (f32[520,128]{1,0:T(8,128)S(1)}, f32[520,128]{1,0:T(8,128)S(1)}, u32[]{:S(2)}, u32[]{:S(2)}) collective-permute-start(f32[520,128]{1,0:T(8,128)S(1)} %get-tuple-element.56), channel_id=1, source_target_pairs={{0,1},{1,0},{2,3},{3,2},{4,5},{5,4},{6,7},{7,6},{8,9},{9,8},{10,11... | collective-permute-start | bytes 798728 | tf_op jit(solution)/shard_map/ppermute | solution.py:391
  18.3 19.8 %copy-start.13 = (s32[2,128]{1,0:T(2,128)S(1)}, s32[2,128]{1,0:T(2,128)}, u32[]{:S(2)}) copy-start(s32[2,128]{1,0:T(2,128)} %lists.3) | copy-start | bytes 3076
  18.3 8.5 %collective-permute-start.3 = (f32[520,128]{1,0:T(8,128)S(1)}, f32[520,128]{1,0:T(8,128)S(1)}, u32[]{:S(2)}, u32[]{:S(2)}) collective-permute-start(f32[520,128]{1,0:T(8,128)S(1)} %add.8.mine._), channel_id=1, source_target_pairs={{0,2},{1,3},{2,0},{3,1},{4,6},{5,7},{6,4},{7,5},{8,10},{9,11},{10,... | collective-permute-start | bytes 798728 | tf_op jit(solution)/shard_map/ppermute | solution.py:391
  26.9 11.1 %collective-permute-start.4 = (f32[512,128]{1,0:T(8,128)S(1)}, f32[512,128]{1,0:T(8,128)S(1)}, u32[]{:S(2)}, u32[]{:S(2)}) collective-permute-start(f32[512,128]{1,0:T(8,128)S(1)} %shard_map.148.mine), channel_id=1, source_target_pairs={{0,1},{1,0},{2,3},{3,2},{4,5},{5,4},{6,7},{7,6},{8,9},{9,8},{10,11... | collective-permute-start | bytes 786440 | tf_op jit(solution)/shard_map/ppermute | solution.py:391
  27.0 6.2 %collective-permute-start.14 = (f32[256,128]{1,0:T(8,128)}, f32[256,128]{1,0:T(8,128)}, u32[]{:S(2)}, u32[]{:S(2)}) collective-permute-start(f32[256,128]{1,0:T(8,128)} %bitcast.10.refs_13_), channel_id=1, source_target_pairs={{0,2},{1,3},{2,0},{3,1},{4,6},{5,7},{6,4},{7,5},{8,10},{9,11},{10,... | collective-permute-start | bytes 393224 | tf_op jit(solution)/shard_map/ppermute | solution.py:391
  27.4 31.5 %collective-permute-start.13 = (f32[256,128]{1,0:T(8,128)}, f32[256,128]{1,0:T(8,128)}, u32[]{:S(2)}, u32[]{:S(2)}) collective-permute-start(f32[256,128]{1,0:T(8,128)} %bitcast.10.refs_13_), channel_id=1, source_target_pairs={{0,1},{1,0},{2,3},{3,2},{4,5},{5,4},{6,7},{7,6},{8,9},{9,8},{10,11... | collective-permute-start | bytes 393224 | tf_op jit(solution)/shard_map/ppermute | solution.py:391
  33.2 25.6 %collective-permute-start.15 = (f32[256,128]{1,0:T(8,128)}, f32[256,128]{1,0:T(8,128)S(1)}, u32[]{:S(2)}, u32[]{:S(2)}) collective-permute-start(f32[256,128]{1,0:T(8,128)} %collective-permute-done.14.refs_15_), channel_id=1, source_target_pairs={{0,1},{1,0},{2,3},{3,2},{4,5},{5,4},{6,7},{7,6},{8,9},{9,8},{10,11... | collective-permute-start | bytes 393224 | tf_op jit(solution)/shard_map/ppermute | solution.py:391
  36.1 6.2 %copy-start.14 = (s32[1024,4]{0,1:T(4,128)S(1)}, s32[1024,4]{0,1:T(4,128)}, u32[]{:S(2)}) copy-start(s32[1024,4]{0,1:T(4,128)} %param.21) | copy-start | bytes 49156
  38.4 6.8 %collective-permute-start.5 = (f32[128,128]{1,0:T(8,128)S(1)}, f32[128,128]{1,0:T(8,128)S(1)}, u32[]{:S(2)}, u32[]{:S(2)}) collective-permute-start(f32[128,128]{1,0:T(8,128)S(1)} %get-tuple-element.58), channel_id=1, source_target_pairs={{0,4},{4,8},{8,12},{12,0},{1,5},{5,9},{9,13},{13,1},{2,6},{6,10},{... | collective-permute-start | bytes 196616 | tf_op jit(solution)/shard_map/ppermute | solution.py:386
  38.6 6.6 %collective-permute-start.6 = (f32[128,128]{1,0:T(8,128)S(1)}, f32[128,128]{1,0:T(8,128)S(1)}, u32[]{:S(2)}, u32[]{:S(2)}) collective-permute-start(f32[128,128]{1,0:T(8,128)S(1)} %get-tuple-element.59), channel_id=1, source_target_pairs={{0,12},{4,0},{8,4},{12,8},{1,13},{5,1},{9,5},{13,9},{2,14},{6,2},{... | collective-permute-start | bytes 196616 | tf_op jit(solution)/shard_map/ppermute | solution.py:386
  47.8 5.2 %collective-permute-start.7 = (f32[128,128]{1,0:T(8,128)S(1)}, f32[128,128]{1,0:T(8,128)S(1)}, u32[]{:S(2)}, u32[]{:S(2)}) collective-permute-start(f32[128,128]{1,0:T(8,128)S(1)} %get-tuple-element.65.refs_0_), channel_id=1, source_target_pairs={{0,12},{4,0},{8,4},{12,8},{1,13},{5,1},{9,5},{13,9},{2,14},{6,2},{... | collective-permute-start | bytes 196616 | tf_op jit(solution)/shard_map/ppermute | solution.py:386
  50.9 5.2 %collective-permute-start.8 = (f32[128,128]{1,0:T(8,128)S(1)}, f32[128,128]{1,0:T(8,128)S(1)}, u32[]{:S(2)}, u32[]{:S(2)}) collective-permute-start(f32[128,128]{1,0:T(8,128)S(1)} %get-tuple-element.65.refs_0_), channel_id=1, source_target_pairs={{0,8},{4,12},{8,0},{12,4},{1,9},{5,13},{9,1},{13,5},{2,10},{6,14},... | collective-permute-start | bytes 196616 | tf_op jit(solution)/shard_map/ppermute | solution.py:386
  51.0 6.1 %collective-permute-start.9 = (f32[128,128]{1,0:T(8,128)S(1)}, f32[128,128]{1,0:T(8,128)S(1)}, u32[]{:S(2)}, u32[]{:S(2)}) collective-permute-start(f32[128,128]{1,0:T(8,128)S(1)} %get-tuple-element.65.refs_0_), channel_id=1, source_target_pairs={{0,4},{4,8},{8,12},{12,0},{1,5},{5,9},{9,13},{13,1},{2,6},{6,10},{... | collective-permute-start | bytes 196616 | tf_op jit(solution)/shard_map/ppermute | solution.py:386
  52.9 5.9 %collective-permute-start.10 = (f32[128,128]{1,0:T(8,128)S(1)}, f32[128,128]{1,0:T(8,128)S(1)}, u32[]{:S(2)}, u32[]{:S(2)}) collective-permute-start(f32[128,128]{1,0:T(8,128)S(1)} %collective-permute-done.7.refs_1_), channel_id=1, source_target_pairs={{0,1},{1,0},{2,3},{3,2},{4,5},{5,4},{6,7},{7,6},{8,9},{9,8},{10,11... | collective-permute-start | bytes 196616 | tf_op jit(solution)/shard_map/ppermute | solution.py:391
  56.1 2.7 %collective-permute-start.11 = (f32[128,128]{1,0:T(8,128)S(1)}, f32[128,128]{1,0:T(8,128)S(1)}, u32[]{:S(2)}, u32[]{:S(2)}) collective-permute-start(f32[128,128]{1,0:T(8,128)S(1)} %collective-permute-done.8.refs_2_), channel_id=1, source_target_pairs={{0,1},{1,0},{2,3},{3,2},{4,5},{5,4},{6,7},{7,6},{8,9},{9,8},{10,11... | collective-permute-start | bytes 196616 | tf_op jit(solution)/shard_map/ppermute | solution.py:391
  57.0 1.9 %collective-permute-start.12 = (f32[128,128]{1,0:T(8,128)S(1)}, f32[128,128]{1,0:T(8,128)S(1)}, u32[]{:S(2)}, u32[]{:S(2)}) collective-permute-start(f32[128,128]{1,0:T(8,128)S(1)} %collective-permute-done.9.refs_3_), channel_id=1, source_target_pairs={{0,1},{1,0},{2,3},{3,2},{4,5},{5,4},{6,7},{7,6},{8,9},{9,8},{10,11... | collective-permute-start | bytes 196616 | tf_op jit(solution)/shard_map/ppermute | solution.py:391
  (7 other events, 26.1 us)
where the time goes:
time: 64.1 us; the launch traced here: 63.8 us
  Pallas kernels  25 us (39%)
  waiting for transfers between devices  21.3 us (33%)
  starting transfers between devices  14 us (22%)
  local copies, waits for them, and re-layouts  2.91 us (5%)
    pallas_call x10, Pallas kernels, run(): pl.pallas_call(kernel, out_shape=outs, grid_spec=pltpu.PrefetchScalarGrid...  25 us
    ppermute x9, waiting for transfers between devices, swapped(): return lax.ppermute(value, axis, [(s, s ^ bit) for s in range(count)])  15.6 us
    ppermute x7, starting transfers between devices, passed(): lax.ppermute(value, axis, [(s, (s + steps) % count) for s in range(count)])  13.2 us
    ppermute x7, waiting for transfers between devices, passed(): lax.ppermute(value, axis, [(s, (s + steps) % count) for s in range(count)])  5.66 us
    unnamed x30, local copies, waits for them, and re-layouts  2.91 us
  transfers between devices with their start and end apart: 16, of which 7 were waited for; matrix products, arithmetic and copies ran while one was open for 0% of the time, Pallas kernels for 23%

commit v1 on v0

--- a/solution.py
+++ b/solution.py
@@ -260,13 +260,13 @@
         chosen[rows, :] = picks(named.astype(jnp.int32).astype(jnp.int16), chosen.shape[1])
 
 
-def mean_kernel(lines, mine, theirs, out):
+def mean_kernel(lines, total, out):
     part = out.shape[0]
-    counts = mine[part : part + lines, :] + theirs[part : part + lines, :]
+    counts = total[part : part + lines, :]
     for r in range(lines):
         rows = slice(r * LANES, (r + 1) * LANES)
         share = 1.0 / jnp.transpose(jnp.broadcast_to(counts[r : r + 1, :], (LANES, LANES)))
-        out[rows, :] = (mine[rows, :] + theirs[rows, :]) * share
+        out[rows, :] = total[rows, :] * share
 
 
 def quarter_nodes_kernel(flip, mine, other, lists, nodes, to_next, to_previous):
@@ -486,7 +486,7 @@
             pl.BlockSpec((c_degree, block), lambda i, place: (0, place[0])), *layer_specs, in_hbm,
         ],
         (quarter_pool_rows, pool_rows, quarter_edges.reshape(q_rows * q_degree, w), coarse_senders,
-         *layers, after),
+         *[hbm(x) for x in layers], after),
         (
             shaped(block, w), shaped(rows, block, dtype=half), shaped(q_degree, q_rows, w), shaped(q_rows, w),
             shaped(c_degree, block, w, dtype=short), shaped(*mats(2), dtype=half), shaped(*mats(4), dtype=half),
@@ -500,7 +500,7 @@
         [], 16, 10**9,
     )
     mine = run(
-        functools.partial(mean_kernel, lines), (1,), (), [whole(part + height, w)] * 2, (mine, theirs),
+        functools.partial(mean_kernel, lines), (1,), (), [whole(part + height, w)], (mine + theirs,),
         shaped(part, w), whole(part, w), [], 6, 10**7,
     )
     other = swapped(mine, "sub", 1)

time: 64.1 us -> 64 us (level)
  Pallas kernels: 25 us -> 26.3 us
  local copies, waits for them, and re-layouts: 2.91 us -> 1.81 us
    pallas_call x10, Pallas kernels: 25 us -> 26.3 us  [run(): pl.pallas_call(kernel, out_shape=outs, grid_spec=pltpu.PrefetchScalarGrid...]
    unnamed x30, local copies, waits for them, and re-layouts: 2.91 us -> 1.81 us
  transfers between devices with their start and end apart: 16 -> 16, of which waited for: 7 -> 7; matrix products, arithmetic and copies ran while one was open for 0% -> 0% of each run, Pallas kernels for 23% -> 26%
where the time goes in v1:
time: 64 us; the launch traced here: 63.7 us
  Pallas kernels  26.3 us (41%)
  waiting for transfers between devices  21 us (33%)
  starting transfers between devices  13.9 us (22%)
  local copies, waits for them, and re-layouts  1.81 us (3%)
    pallas_call x10, Pallas kernels, run(): pl.pallas_call(kernel, out_shape=outs, grid_spec=pltpu.PrefetchScalarGrid...  26.3 us
    ppermute x9, waiting for transfers between devices, swapped(): return lax.ppermute(value, axis, [(s, s ^ bit) for s in range(count)])  15.4 us
    ppermute x7, starting transfers between devices, passed(): lax.ppermute(value, axis, [(s, (s + steps) % count) for s in range(count)])  13.1 us
    ppermute x7, waiting for transfers between devices, passed(): lax.ppermute(value, axis, [(s, (s + steps) % count) for s in range(count)])  5.65 us
    unnamed x30, local copies, waits for them, and re-layouts  1.81 us
  transfers between devices with their start and end apart: 16, of which 7 were waited for; matrix products, arithmetic and copies ran while one was open for 0% of the time, Pallas kernels for 26%

profile of v1, /device:TPU:0, one launch (start us, length us, event | category | flops | bytes accessed | tf_op | source)
XLA Modules:
  0.0 63.7 jit_solution(4193509826422010422)
XLA Ops:
  0.0 1.5 %shard_map.145 = (f32[128,128]{1,0:T(8,128)S(1)}, f32[128,128]{1,0:T(8,128)S(1)}, f32[1024,128]{1,0:T(8,128)S(1)}, s32[6,1024]{1,0:T(8,128)S(1)}, s32[8,128]{1,0...) custom-call(s32[2,128]{1,0:T(2,128)} %lists.2, ...), custom_call_target="tpu_custom_call" | custom-call | flops 100000000 | bytes 1000000 | tf_op jit(solution)/shard_map/pallas_call | solution.py:372
  1.5 0.7 %copy-done.11 = bf16[3,256,256]{2,1,0:T(8,128)(2,1)} copy-done((bf16[3,256,256]{2,1,0:T(8,128)(2,1)}, bf16[3,256,256]{2,1,0:T(8,128)(2,1)S(1)}, u32[]{:S(2)}) %copy-start.11) | copy-done | bytes 393240
  2.3 0.5 collective-permute-start
  2.8 5.0 %collective-permute-start.1 = (f32[128,128]{1,0:T(8,128)S(1)}, f32[128,128]{1,0:T(8,128)S(1)}, u32[]{:S(2)}, u32[]{:S(2)}) collective-permute-start(f32[128,128]{1,0:T(8,128)S(1)} %get-tuple-element.40), channel_id=1, source_target_pairs={{0,15},{1,0},{2,1},{3,2},{4,3},{5,4},{6,5},{7,6},{8,7},{9,8},{10,9... | collective-permute-start | bytes 196616 | tf_op jit(solution)/shard_map/ppermute | solution.py:386
  7.7 1.0 %copy-done.12 = bf16[3,256,256]{2,1,0:T(8,128)(2,1)S(1)} copy-done((bf16[3,256,256]{2,1,0:T(8,128)(2,1)S(1)}, bf16[3,256,256]{2,1,0:T(8,128)(2,1)}, u32[]{:S(2)}) %copy-start.12) | copy-done | bytes 393240
  8.8 5.7 %shard_map.146 = (f32[1024,128]{1,0:T(8,128)S(1)}, f32[1024,128]{1,0:T(8,128)S(1)}, f32[1024,128]{1,0:T(8,128)S(1)}, f32[1024,128]{1,0:T(8,128)S(1)}, f32[1024,1...) custom-call(s32[1]{0:T(128)} %bitcast.1.flip, ...), custom_call_target="tpu_custom_call" | custom-call | flops 8000000000 | bytes 1000000 | tf_op jit(solution)/shard_map/pallas_call | solution.py:372
  14.6 3.6 %shard_map.147 = (f32[1024,128]{1,0:T(8,128)}, f32[520,128]{1,0:T(8,128)S(1)}, f32[520,128]{1,0:T(8,128)S(1)}) custom-call(s32[1]{0:T(128)} %bitcast.1.flip, s32[6,1024]{1,0:T(8,128)S(1)} %bitcast.13, s32[8,128]{1,0:T(8,128)S(1)} %bitcast.16, f32[1024,128]{1,0:T(8,128)S(1)} %copy-done.2, f32[128,128]{1,0:T(8,128)S(1)} %collective-permute-done.left, ...), custom_call_target="tpu_custom_call" | custom-call | flops 4000000000 | bytes 1000000 | tf_op jit(solution)/shard_map/pallas_call | solution.py:372
  18.3 1.5 %collective-permute-done.2 = f32[520,128]{1,0:T(8,128)S(1)} collective-permute-done((f32[520,128]{1,0:T(8,128)S(1)}, f32[520,128]{1,0:T(8,128)S(1)}, u32[]{:S(2)}, u32[]{:S(2)}) %collective-permute-start.2) | collective-permute-done | bytes 266272 | tf_op jit(solution)/shard_map/ppermute | solution.py:391
  20.0 8.4 %collective-permute-done.3 = f32[520,128]{1,0:T(8,128)S(1)} collective-permute-done((f32[520,128]{1,0:T(8,128)S(1)}, f32[520,128]{1,0:T(8,128)S(1)}, u32[]{:S(2)}, u32[]{:S(2)}) %collective-permute-start.3) | collective-permute-done | bytes 266272 | tf_op jit(solution)/shard_map/ppermute | solution.py:391
  28.7 0.4 collective-permute-start.14
  29.3 5.4 %collective-permute-done.14.refs_15_ = f32[256,128]{1,0:T(8,128)} collective-permute-done((f32[256,128]{1,0:T(8,128)S(1)}, f32[256,128]{1,0:T(8,128)}, u32[]{:S(2)}, u32[]{:S(2)}) %collective-permute-start.14) | collective-permute-done | bytes 131104 | tf_op jit(solution)/shard_map/ppermute | solution.py:391
  34.7 3.3 %shard_map.150 = (f32[256,128]{1,0:T(8,128)S(1)}, bf16[1024,256]{1,0:T(8,128)(2,1)S(1)}, f32[4,1024,128]{2,1,0:T(8,128)S(1)}, f32[1024,128]{1,0:T(8,128)S(1)}, s...) custom-call(s32[2]{0:T(128)S(1)} %pad_add_fusion.1.flip, ...), custom_call_target="tpu_custom_call" | custom-call | flops 1000000000 | bytes 1000000 | tf_op jit(solution)/shard_map/pallas_call | solution.py:372
  38.0 0.4 shard_map.149
  38.7 3.6 %collective-permute-start.6 = (f32[128,128]{1,0:T(8,128)S(1)}, f32[128,128]{1,0:T(8,128)S(1)}, u32[]{:S(2)}, u32[]{:S(2)}) collective-permute-start(f32[128,128]{1,0:T(8,128)S(1)} %get-tuple-element.59), channel_id=1, source_target_pairs={{0,12},{4,0},{8,4},{12,8},{1,13},{5,1},{9,5},{13,9},{2,14},{6,2},{... | collective-permute-start | bytes 196616 | tf_op jit(solution)/shard_map/ppermute | solution.py:386
  42.2 2.6 %shard_map.151.before = f32[4,1024,128]{2,1,0:T(8,128)S(1)} custom-call(s32[4,1024]{1,0:T(4,128)S(1)} %bitcast.24, f32[1024,128]{1,0:T(8,128)S(1)} %get-tuple-element.57.nodes, f32[4,1024,128]{2,1,0:T(8,128)S(1)} %get-tuple-element.60.extra, bf16[2,256,256]{2,1,0:T(8,128)(2,1)S(1)} %get-tuple-element.61.weights.first_weights), custom_call_target="tpu_custom_call" | custom-call | flops 3000000000 | bytes 1000000 | tf_op jit(solution)/shard_map/pallas_call | solution.py:372
  44.9 0.3 collective-permute-done.5.left
  45.2 2.6 %shard_map.152 = (f32[1024,128]{1,0:T(8,128)S(1)}, f32[128,128]{1,0:T(8,128)S(1)}, f32[128,128]{1,0:T(8,128)S(1)}) custom-call(s32[1]{0:T(128)} %bitcast.1.flip, s32[4,1024]{1,0:T(4,128)S(1)} %bitcast.25, s32[8,128]{1,0:T(8,128)S(1)} %bitcast.20, f32[1024,128]{1,0:T(8,128)S(1)} %get-tuple-element.57.nodes, f32[128,128]{1,0:T(8,128)S(1)} %collective-permute-done.5.left, ...), custom_call_target="tpu_custom_call" | custom-call | flops 2000000000 | bytes 1000000 | tf_op jit(solution)/shard_map/pallas_call | solution.py:372
  47.8 3.2 %collective-permute-start.7 = (f32[128,128]{1,0:T(8,128)S(1)}, f32[128,128]{1,0:T(8,128)S(1)}, u32[]{:S(2)}, u32[]{:S(2)}) collective-permute-start(f32[128,128]{1,0:T(8,128)S(1)} %get-tuple-element.65.refs_0_), channel_id=1, source_target_pairs={{0,12},{4,0},{8,4},{12,8},{1,13},{5,1},{9,5},{13,9},{2,14},{6,2},{... | collective-permute-start | bytes 196616 | tf_op jit(solution)/shard_map/ppermute | solution.py:386
  50.9 0.6 %collective-permute-start.9 = (f32[128,128]{1,0:T(8,128)S(1)}, f32[128,128]{1,0:T(8,128)S(1)}, u32[]{:S(2)}, u32[]{:S(2)}) collective-permute-start(f32[128,128]{1,0:T(8,128)S(1)} %get-tuple-element.65.refs_0_), channel_id=1, source_target_pairs={{0,4},{4,8},{8,12},{12,0},{1,5},{5,9},{9,13},{13,1},{2,6},{6,10},{... | collective-permute-start | bytes 196616 | tf_op jit(solution)/shard_map/ppermute | solution.py:386
  51.7 1.3 %collective-permute-done.7.refs_1_ = f32[128,128]{1,0:T(8,128)S(1)} collective-permute-done((f32[128,128]{1,0:T(8,128)S(1)}, f32[128,128]{1,0:T(8,128)S(1)}, u32[]{:S(2)}, u32[]{:S(2)}) %collective-permute-start.7) | collective-permute-done | bytes 65568 | tf_op jit(solution)/shard_map/ppermute | solution.py:386
  52.9 3.2 %collective-permute-done.8.refs_2_ = f32[128,128]{1,0:T(8,128)S(1)} collective-permute-done((f32[128,128]{1,0:T(8,128)S(1)}, f32[128,128]{1,0:T(8,128)S(1)}, u32[]{:S(2)}, u32[]{:S(2)}) %collective-permute-start.8) | collective-permute-done | bytes 65568 | tf_op jit(solution)/shard_map/ppermute | solution.py:386
  56.1 0.9 %collective-permute-done.9.refs_3_ = f32[128,128]{1,0:T(8,128)S(1)} collective-permute-done((f32[128,128]{1,0:T(8,128)S(1)}, f32[128,128]{1,0:T(8,128)S(1)}, u32[]{:S(2)}, u32[]{:S(2)}) %collective-permute-start.9) | collective-permute-done | bytes 65568 | tf_op jit(solution)/shard_map/ppermute | solution.py:386
  57.0 1.8 %shard_map.153.refs_10_ = f32[1024,128]{1,0:T(8,128)S(1)} custom-call(s32[8,128]{1,0:T(8,128)S(1)} %bitcast.18, f32[1024,128]{1,0:T(8,128)S(1)} %get-tuple-element.69.quarter, f32[1024,128]{1,0:T(8,128)} %get-tuple-element.70.fine_new), custom_call_target="tpu_custom_call" | custom-call | flops 1000000000 | bytes 1000000 | tf_op jit(solution)/shard_map/pallas_call | solution.py:372
  58.9 4.7 %shard_map.154 = f32[1024,128]{1,0:T(8,128)} custom-call(s32[3]{0:T(128)S(1)} %pad_add_fusion.place, f32[128,128]{1,0:T(8,128)S(1)} %get-tuple-element.65.refs_0_, f32[128,128]{1,0:T(8,128)S(1)} %collective-permute-done.7.refs_1_, f32[128,128]{1,0:T(8,128)S(1)} %collective-permute-done.8.refs_2_, f32[128,128]{1,0:T(8,128)S(1)} %collective-permute-done.9.refs_3_, ...), custom_call_target="tpu_custom_call" | custom-call | flops 2000000000 | bytes 1000000 | tf_op jit(solution)/shard_map/pallas_call | solution.py:372
  (52 shorter events, 1.1 us)
Async XLA Ops:
  2.3 12.2 %collective-permute-start = (f32[128,128]{1,0:T(8,128)S(1)}, f32[128,128]{1,0:T(8,128)S(1)}, u32[]{:S(2)}, u32[]{:S(2)}) collective-permute-start(f32[128,128]{1,0:T(8,128)S(1)} %get-tuple-element.39), channel_id=1, source_target_pairs={{0,1},{1,2},{2,3},{3,4},{4,5},{5,6},{6,7},{7,8},{8,9},{9,10},{10,1... | collective-permute-start | bytes 196616 | tf_op jit(solution)/shard_map/ppermute | solution.py:386
  2.8 11.7 %collective-permute-start.1 = (f32[128,128]{1,0:T(8,128)S(1)}, f32[128,128]{1,0:T(8,128)S(1)}, u32[]{:S(2)}, u32[]{:S(2)}) collective-permute-start(f32[128,128]{1,0:T(8,128)S(1)} %get-tuple-element.40), channel_id=1, source_target_pairs={{0,15},{1,0},{2,1},{3,2},{4,3},{5,4},{6,5},{7,6},{8,7},{9,8},{10,9... | collective-permute-start | bytes 196616 | tf_op jit(solution)/shard_map/ppermute | solution.py:386
  8.7 5.8 %copy-start.5 = (f32[3,128,128]{2,1,0:T(8,128)S(1)}, f32[3,128,128]{2,1,0:T(8,128)}, u32[]{:S(2)}) copy-start(f32[3,128,128]{2,1,0:T(8,128)} %node_out.1) | copy-start | bytes 589828
  8.7 5.8 %copy-start.6 = (s32[1024,6]{0,1:T(8,128)S(1)}, s32[1024,6]{0,1:T(8,128)}, u32[]{:S(2)}) copy-start(s32[1024,6]{0,1:T(8,128)} %param.17) | copy-start | bytes 73732
  14.6 14.1 %copy-start.13 = (f32[64,4,128]{2,1,0:T(4,128)S(1)}, f32[64,4,128]{2,1,0:T(4,128)}, u32[]{:S(2)}) copy-start(f32[64,4,128]{2,1,0:T(4,128)} %param.24) | copy-start | bytes 393220
  18.2 16.5 %copy-start.1 = (f32[1024,4,128]{2,1,0:T(4,128)S(1)}, f32[1024,4,128]{2,1,0:T(4,128)}, u32[]{:S(2)}) copy-start(f32[1024,4,128]{2,1,0:T(4,128)} %param.20) | copy-start | bytes 6291460
  18.2 16.5 %copy-start.7 = (s32[1024,4]{0,1:T(4,128)S(1)}, s32[1024,4]{0,1:T(4,128)}, u32[]{:S(2)}) copy-start(s32[1024,4]{0,1:T(4,128)} %param.25) | copy-start | bytes 49156
  18.2 16.5 %copy-start.9 = (s32[1024]{0:T(1024)S(1)}, s32[1024]{0:T(1024)}, u32[]{:S(2)}) copy-start(s32[1024]{0:T(1024)} %param.23) | copy-start | bytes 12292
  18.3 1.6 %collective-permute-start.2 = (f32[520,128]{1,0:T(8,128)S(1)}, f32[520,128]{1,0:T(8,128)S(1)}, u32[]{:S(2)}, u32[]{:S(2)}) collective-permute-start(f32[520,128]{1,0:T(8,128)S(1)} %get-tuple-element.56), channel_id=1, source_target_pairs={{0,1},{1,0},{2,3},{3,2},{4,5},{5,4},{6,7},{7,6},{8,9},{9,8},{10,11... | collective-permute-start | bytes 798728 | tf_op jit(solution)/shard_map/ppermute | solution.py:391
  19.9 8.5 %collective-permute-start.3 = (f32[520,128]{1,0:T(8,128)S(1)}, f32[520,128]{1,0:T(8,128)S(1)}, u32[]{:S(2)}, u32[]{:S(2)}) collective-permute-start(f32[520,128]{1,0:T(8,128)S(1)} %add.11._), channel_id=1, source_target_pairs={{0,2},{1,3},{2,0},{3,1},{4,6},{5,7},{6,4},{7,5},{8,10},{9,11},{10,... | collective-permute-start | bytes 798728 | tf_op jit(solution)/shard_map/ppermute | solution.py:391
  28.4 9.6 %copy-start.10 = (s32[2,128]{1,0:T(2,128)S(1)}, s32[2,128]{1,0:T(2,128)}, u32[]{:S(2)}) copy-start(s32[2,128]{1,0:T(2,128)} %lists.3) | copy-start | bytes 3076
  28.6 9.4 %collective-permute-start.4 = (f32[512,128]{1,0:T(8,128)S(1)}, f32[512,128]{1,0:T(8,128)S(1)}, u32[]{:S(2)}, u32[]{:S(2)}) collective-permute-start(f32[512,128]{1,0:T(8,128)S(1)} %shard_map.148.mine), channel_id=1, source_target_pairs={{0,1},{1,0},{2,3},{3,2},{4,5},{5,4},{6,7},{7,6},{8,9},{9,8},{10,11... | collective-permute-start | bytes 786440 | tf_op jit(solution)/shard_map/ppermute | solution.py:391
  28.7 6.0 %collective-permute-start.14 = (f32[256,128]{1,0:T(8,128)S(1)}, f32[256,128]{1,0:T(8,128)}, u32[]{:S(2)}, u32[]{:S(2)}) collective-permute-start(f32[256,128]{1,0:T(8,128)S(1)} %bitcast.21), channel_id=1, source_target_pairs={{0,2},{1,3},{2,0},{3,1},{4,6},{5,7},{6,4},{7,5},{8,10},{9,11},{10,... | collective-permute-start | bytes 393224 | tf_op jit(solution)/shard_map/ppermute | solution.py:391
  29.0 29.8 %collective-permute-start.13 = (f32[256,128]{1,0:T(8,128)S(1)}, f32[256,128]{1,0:T(8,128)}, u32[]{:S(2)}, u32[]{:S(2)}) collective-permute-start(f32[256,128]{1,0:T(8,128)S(1)} %bitcast.22), channel_id=1, source_target_pairs={{0,1},{1,0},{2,3},{3,2},{4,5},{5,4},{6,7},{7,6},{8,9},{9,8},{10,11... | collective-permute-start | bytes 393224 | tf_op jit(solution)/shard_map/ppermute | solution.py:391
  34.7 24.1 %collective-permute-start.15 = (f32[256,128]{1,0:T(8,128)}, f32[256,128]{1,0:T(8,128)S(1)}, u32[]{:S(2)}, u32[]{:S(2)}) collective-permute-start(f32[256,128]{1,0:T(8,128)} %collective-permute-done.14.refs_15_), channel_id=1, source_target_pairs={{0,1},{1,0},{2,3},{3,2},{4,5},{5,4},{6,7},{7,6},{8,9},{9,8},{10,11... | collective-permute-start | bytes 393224 | tf_op jit(solution)/shard_map/ppermute | solution.py:391
  34.7 7.5 %copy-start.14 = (s32[1024,4]{0,1:T(4,128)S(1)}, s32[1024,4]{0,1:T(4,128)}, u32[]{:S(2)}) copy-start(s32[1024,4]{0,1:T(4,128)} %param.21) | copy-start | bytes 49156
  38.4 6.8 %collective-permute-start.5 = (f32[128,128]{1,0:T(8,128)S(1)}, f32[128,128]{1,0:T(8,128)S(1)}, u32[]{:S(2)}, u32[]{:S(2)}) collective-permute-start(f32[128,128]{1,0:T(8,128)S(1)} %get-tuple-element.58), channel_id=1, source_target_pairs={{0,4},{4,8},{8,12},{12,0},{1,5},{5,9},{9,13},{13,1},{2,6},{6,10},{... | collective-permute-start | bytes 196616 | tf_op jit(solution)/shard_map/ppermute | solution.py:386
  38.7 6.5 %collective-permute-start.6 = (f32[128,128]{1,0:T(8,128)S(1)}, f32[128,128]{1,0:T(8,128)S(1)}, u32[]{:S(2)}, u32[]{:S(2)}) collective-permute-start(f32[128,128]{1,0:T(8,128)S(1)} %get-tuple-element.59), channel_id=1, source_target_pairs={{0,12},{4,0},{8,4},{12,8},{1,13},{5,1},{9,5},{13,9},{2,14},{6,2},{... | collective-permute-start | bytes 196616 | tf_op jit(solution)/shard_map/ppermute | solution.py:386
  47.8 5.2 %collective-permute-start.7 = (f32[128,128]{1,0:T(8,128)S(1)}, f32[128,128]{1,0:T(8,128)S(1)}, u32[]{:S(2)}, u32[]{:S(2)}) collective-permute-start(f32[128,128]{1,0:T(8,128)S(1)} %get-tuple-element.65.refs_0_), channel_id=1, source_target_pairs={{0,12},{4,0},{8,4},{12,8},{1,13},{5,1},{9,5},{13,9},{2,14},{6,2},{... | collective-permute-start | bytes 196616 | tf_op jit(solution)/shard_map/ppermute | solution.py:386
  50.9 5.2 %collective-permute-start.8 = (f32[128,128]{1,0:T(8,128)S(1)}, f32[128,128]{1,0:T(8,128)S(1)}, u32[]{:S(2)}, u32[]{:S(2)}) collective-permute-start(f32[128,128]{1,0:T(8,128)S(1)} %get-tuple-element.65.refs_0_), channel_id=1, source_target_pairs={{0,8},{4,12},{8,0},{12,4},{1,9},{5,13},{9,1},{13,5},{2,10},{6,14},... | collective-permute-start | bytes 196616 | tf_op jit(solution)/shard_map/ppermute | solution.py:386
  50.9 6.1 %collective-permute-start.9 = (f32[128,128]{1,0:T(8,128)S(1)}, f32[128,128]{1,0:T(8,128)S(1)}, u32[]{:S(2)}, u32[]{:S(2)}) collective-permute-start(f32[128,128]{1,0:T(8,128)S(1)} %get-tuple-element.65.refs_0_), channel_id=1, source_target_pairs={{0,4},{4,8},{8,12},{12,0},{1,5},{5,9},{9,13},{13,1},{2,6},{6,10},{... | collective-permute-start | bytes 196616 | tf_op jit(solution)/shard_map/ppermute | solution.py:386
  52.9 5.9 %collective-permute-start.10 = (f32[128,128]{1,0:T(8,128)S(1)}, f32[128,128]{1,0:T(8,128)S(1)}, u32[]{:S(2)}, u32[]{:S(2)}) collective-permute-start(f32[128,128]{1,0:T(8,128)S(1)} %collective-permute-done.7.refs_1_), channel_id=1, source_target_pairs={{0,1},{1,0},{2,3},{3,2},{4,5},{5,4},{6,7},{7,6},{8,9},{9,8},{10,11... | collective-permute-start | bytes 196616 | tf_op jit(solution)/shard_map/ppermute | solution.py:391
  56.1 2.7 %collective-permute-start.11 = (f32[128,128]{1,0:T(8,128)S(1)}, f32[128,128]{1,0:T(8,128)S(1)}, u32[]{:S(2)}, u32[]{:S(2)}) collective-permute-start(f32[128,128]{1,0:T(8,128)S(1)} %collective-permute-done.8.refs_2_), channel_id=1, source_target_pairs={{0,1},{1,0},{2,3},{3,2},{4,5},{5,4},{6,7},{7,6},{8,9},{9,8},{10,11... | collective-permute-start | bytes 196616 | tf_op jit(solution)/shard_map/ppermute | solution.py:391
  57.0 1.9 %collective-permute-start.12 = (f32[128,128]{1,0:T(8,128)S(1)}, f32[128,128]{1,0:T(8,128)S(1)}, u32[]{:S(2)}, u32[]{:S(2)}) collective-permute-start(f32[128,128]{1,0:T(8,128)S(1)} %collective-permute-done.9.refs_3_), channel_id=1, source_target_pairs={{0,1},{1,0},{2,3},{3,2},{4,5},{5,4},{6,7},{7,6},{8,9},{9,8},{10,11... | collective-permute-start | bytes 196616 | tf_op jit(solution)/shard_map/ppermute | solution.py:391
  (7 other events, 30.8 us)

commit v2 on v1

--- a/solution.py
+++ b/solution.py
@@ -189,8 +189,8 @@
     counts[:lines, :] = along_lanes(pool, flip[0] * part, lines)
     counts[height : height + lines, :] = along_lanes(pool, (1 - flip[0]) * part, lines)
     for k in range(degree):
-        if k == ready:
-            for copy in copies:
+        if k in (ready, ready + 2):
+            for copy in copies[:2] if k == ready else copies[2:]:
                 copy.wait()
         column = down(senders[k : k + 1, :])
         edge = here[k][...] if k < ready else local[k - ready]
@@ -316,37 +316,53 @@
     out[...] = fine_new[...] + folded(times(picks(column, both.shape[0]), both))
 
 
-def coarse_kernel(n_patch, tile, place, *refs):
-    mine, refs = refs[:n_patch], refs[n_patch:]
-    other, refs = refs[:n_patch], refs[n_patch:]
-    (columns, chosen, base, first_weights, weights), refs = refs[:5], refs[5:]
-    pieces, (out, nodes, edges, wide, new, held, sent) = refs[:-7], refs[-7:]
-    part, w = mine[0].shape
+def coarse_first_kernel(place, own, partner, columns, first_weights, *refs):
+    pieces, (before, edge_sum, nodes, edges, wide) = refs[:-5], refs[-5:]
+    part, w = own.shape
     block = 2 * part
     piece = pieces[0].shape[0]
     degree = columns.shape[0]
-    sources = nodes.shape[0]
     for j, source in enumerate(pieces):
         at = jnp.bitwise_xor(place[2], j)
         edges[pl.ds(pl.multiple_of(at * piece, piece), piece), :] = source[...]
-    for j in range(n_patch):
-        at = lax.rem(place[0] + j, n_patch) * block
-        nodes[pl.ds(pl.multiple_of(at + place[1] * part, part), part), :] = mine[j][...]
-        nodes[pl.ds(pl.multiple_of(at + (1 - place[1]) * part, part), part), :] = other[j][...]
-    wide[:sources, :] = side(folded(times(side(nodes[...]), first_weights[0])))
-    wide[sources:, :] = first_weights[2]
-    for t in range(block // tile):
-        span = slice(t * tile, (t + 1) * tile)
-        receivers = nodes[pl.ds(pl.multiple_of(place[0] * block + t * tile, tile), tile), :]
-        reach = folded(times(side(receivers), first_weights[1]))
-        edge = [edges[pl.ds(t * tile * degree + k, tile, stride=degree), :] for k in range(degree)]
-        operand = [jnp.concatenate([picks(columns[k, span, :], sources), side(edge[k])], axis=1) for k in range(degree)]
-        sums = folded(times(jnp.concatenate(operand, axis=0), wide[...])).reshape(degree, tile, w)
-        hidden = jnp.maximum(sums + reach[None], 0.0).reshape(degree * tile, w)
-        total = edge[0]
-        for k in range(1, degree):
-            total = total + edge[k]
-        new[span, :] = second_part(degree, tile, hidden, total, receivers, weights)
+    nodes[pl.ds(pl.multiple_of(place[1] * part, part), part), :] = own[...]
+    nodes[pl.ds(pl.multiple_of((1 - place[1]) * part, part), part), :] = partner[...]
+    both = side(nodes[...])
+    wide[:block, :] = side(folded(times(both, first_weights[0])))
+    wide[block:, :] = first_weights[2]
+    reach = folded(times(both, first_weights[1]))
+    first = (place[0] * block).astype(jnp.int16)
+    edge = [edges[pl.ds(k, block, stride=degree), :] for k in range(degree)]
+    operand = [jnp.concatenate([picks(columns[k] - first, block), side(edge[k])], axis=1) for k in range(degree)]
+    sums = folded(times(jnp.concatenate(operand, axis=0), wide[...])).reshape(degree, block, w)
+    total = edge[0]
+    for k in range(1, degree):
+        total = total + edge[k]
+    edge_sum[...] = total
+    for k in range(degree):
+        before[k] = sums[k] + reach
+
+
+def coarse_kernel(n_patch, place, own, own_partner, *refs):
+    mine, refs = refs[: n_patch - 1], refs[n_patch - 1 :]
+    other, refs = refs[: n_patch - 1], refs[n_patch - 1 :]
+    columns, chosen, base, before, edge_sum, first_weights, weights, out, nodes, receivers, wide, new, held, sent = refs
+    part, w = own.shape
+    block = 2 * part
+    degree = columns.shape[0]
+    sources = nodes.shape[0]
+    for j in range(n_patch - 1):
+        nodes[pl.ds(pl.multiple_of(j * block + place[1] * part, part), part), :] = mine[j][...]
+        nodes[pl.ds(pl.multiple_of(j * block + (1 - place[1]) * part, part), part), :] = other[j][...]
+    receivers[pl.ds(pl.multiple_of(place[1] * part, part), part), :] = own[...]
+    receivers[pl.ds(pl.multiple_of((1 - place[1]) * part, part), part), :] = own_partner[...]
+    wide[...] = side(folded(times(side(nodes[...]), first_weights[0])))
+    first = ((place[0] + 1) * block).astype(jnp.int16)
+    column = columns[...] - first
+    column = jnp.where(column < 0, column + jnp.int16(n_patch * block), column)
+    operand = jnp.concatenate([picks(column[k], sources) for k in range(degree)], axis=0)
+    hidden = jnp.maximum(folded(times(operand, wide[...])) + before[...].reshape(degree * block, w), 0.0)
+    new[...] = second_part(degree, block, hidden, edge_sum[...], receivers[...], weights)
     both = side(new[...])
     steps = sent.shape[0]
     rows = out.shape[0] // steps
@@ -405,7 +421,6 @@
     block = total // n_patch
     part, c_part = q_rows // 2, block // 2
     tile = min(512, q_rows)
-    c_tile = min(256, block)
     lines = part // LANES
     height = -(-lines // 8) * 8
     core = sub % 2
@@ -546,17 +561,33 @@
         base_kernel, (1,), (), [whole(*pool_rows.shape), whole(q_rows, w), whole(rows, w)],
         (pool_rows, quarter_new, hbm(fine_new)), shaped(rows, w), whole(rows, w), [], 16, 10**9,
     )
+    place = jnp.stack([patch, core, sub])
+    before, edge_sum = run(
+        coarse_first_kernel, (1,), (place,),
+        [
+            whole(c_part, w), whole(c_part, w), whole(c_degree, block, w), whole(*mats(3)),
+            *[whole(*own_edges.shape)] * n_sub,
+        ],
+        (own, own_partner, coarse_columns, coarse_weights, *edge_pieces),
+        (shaped(c_degree, block, w), shaped(block, w)), [whole(c_degree, block, w), whole(block, w)],
+        [
+            pltpu.VMEM((block, w), f32), pltpu.VMEM((block * c_degree, w), f32),
+            pltpu.VMEM((block + 2 * w, 2 * w), half),
+        ],
+        16, 10**9,
+    )
     return run(
-        functools.partial(coarse_kernel, n_patch, c_tile), (1,), (jnp.stack([patch, core, sub]),),
+        functools.partial(coarse_kernel, n_patch), (1,), (place,),
         [
             *[whole(c_part, w)] * (2 * n_patch), whole(c_degree, block, w), whole(rows, block), whole(rows, w),
-            whole(*mats(3)), whole(*mats(4)), *[whole(*own_edges.shape)] * n_sub,
-        ],
-        (*pieces, *partner, coarse_columns, chosen, base, coarse_weights, coarse_later, *edge_pieces),
+            whole(c_degree, block, w), whole(block, w), whole(*mats(3)), whole(*mats(4)),
+        ],
+        (own, own_partner, *pieces[1:], *partner[1:], coarse_columns, chosen, base, before, edge_sum, coarse_weights,
+         coarse_later),
         shaped(rows, w), in_hbm,
         [
-            pltpu.VMEM((total, w), f32), pltpu.VMEM((block * c_degree, w), f32),
-            pltpu.VMEM((total + 2 * w, 2 * w), half), pltpu.VMEM((block, w), f32), pltpu.VMEM((rows, w), f32),
+            pltpu.VMEM((total - block, w), f32), pltpu.VMEM((block, w), f32),
+            pltpu.VMEM((total - block, 2 * w), half), pltpu.VMEM((block, w), f32), pltpu.VMEM((rows, w), f32),
             pltpu.SemaphoreType.DMA((4,)),
         ],
         big, 2 * 10**9,

time: 64 us -> 58 us (0.906)
  waiting for transfers between devices: 21 us -> 14.2 us
  starting transfers between devices: 13.9 us -> 15.4 us
  Pallas kernels: 26.3 us -> 25.4 us
    ppermute x9, waiting for transfers between devices: 15.4 us -> 10.4 us  [swapped(): return lax.ppermute(value, axis, [(s, s ^ bit) for s in range(count)])]
    ppermute x7, waiting for transfers between devices: 5.65 us -> 3.84 us  [passed(): lax.ppermute(value, axis, [(s, (s + steps) % count) for s in range(count)])]
    ppermute x9, starting transfers between devices: 0.72 us -> 2.3 us  [swapped(): return lax.ppermute(value, axis, [(s, s ^ bit) for s in range(count)])]
    pallas_call x10 -> x11, Pallas kernels: 26.3 us -> 25.4 us  [run(): pl.pallas_call(kernel, out_shape=outs, grid_spec=pltpu.PrefetchScalarGrid...]
  transfers between devices with their start and end apart: 16 -> 16, of which waited for: 7 -> 7; matrix products, arithmetic and copies ran while one was open for 0% -> 0% of each run, Pallas kernels for 26% -> 29%
where the time goes in v2:
time: 58 us; the launch traced here: 57.7 us
  Pallas kernels  25.4 us (44%)
  starting transfers between devices  15.4 us (27%)
  waiting for transfers between devices  14.2 us (24%)
  local copies, waits for them, and re-layouts  1.9 us (3%)
    pallas_call x11, Pallas kernels, run(): pl.pallas_call(kernel, out_shape=outs, grid_spec=pltpu.PrefetchScalarGrid...  25.4 us
    ppermute x7, starting transfers between devices, passed(): lax.ppermute(value, axis, [(s, (s + steps) % count) for s in range(count)])  13.1 us
    ppermute x9, waiting for transfers between devices, swapped(): return lax.ppermute(value, axis, [(s, s ^ bit) for s in range(count)])  10.4 us
    ppermute x7, waiting for transfers between devices, passed(): lax.ppermute(value, axis, [(s, (s + steps) % count) for s in range(count)])  3.84 us
    ppermute x9, starting transfers between devices, swapped(): return lax.ppermute(value, axis, [(s, s ^ bit) for s in range(count)])  2.3 us
    unnamed x30, local copies, waits for them, and re-layouts  1.9 us
  transfers between devices with their start and end apart: 16, of which 7 were waited for; matrix products, arithmetic and copies ran while one was open for 0% of the time, Pallas kernels for 29%

profile of v2, /device:TPU:0, one launch (start us, length us, event | category | flops | bytes accessed | tf_op | source)
XLA Modules:
  0.0 57.7 jit_solution(8799879149035935636)
XLA Ops:
  0.0 1.5 %shard_map.145 = (f32[128,128]{1,0:T(8,128)S(1)}, f32[128,128]{1,0:T(8,128)S(1)}, f32[1024,128]{1,0:T(8,128)S(1)}, s32[6,1024]{1,0:T(8,128)S(1)}, s32[8,128]{1,0...) custom-call(s32[2,128]{1,0:T(2,128)} %lists.2, ...), custom_call_target="tpu_custom_call" | custom-call | flops 100000000 | bytes 1000000 | tf_op jit(solution)/shard_map/pallas_call | solution.py:388
  1.5 0.8 %copy-done.11 = f32[1024,128]{1,0:T(8,128)} copy-done((f32[1024,128]{1,0:T(8,128)}, f32[1024,128]{1,0:T(8,128)S(1)}, u32[]{:S(2)}) %copy-start.11) | copy-done | bytes 524312
  2.3 0.5 collective-permute-start
  2.8 5.0 %collective-permute-start.1 = (f32[128,128]{1,0:T(8,128)S(1)}, f32[128,128]{1,0:T(8,128)S(1)}, u32[]{:S(2)}, u32[]{:S(2)}) collective-permute-start(f32[128,128]{1,0:T(8,128)S(1)} %get-tuple-element.42), channel_id=1, source_target_pairs={{0,15},{1,0},{2,1},{3,2},{4,3},{5,4},{6,5},{7,6},{8,7},{9,8},{10,9... | collective-permute-start | bytes 196616 | tf_op jit(solution)/shard_map/ppermute | solution.py:402
  7.8 1.0 %copy-done.12 = f32[1024,128]{1,0:T(8,128)S(1)} copy-done((f32[1024,128]{1,0:T(8,128)S(1)}, f32[1024,128]{1,0:T(8,128)}, u32[]{:S(2)}) %copy-start.12) | copy-done | bytes 524312
  8.9 5.1 %shard_map.146 = (f32[1024,128]{1,0:T(8,128)S(1)}, f32[1024,128]{1,0:T(8,128)S(1)}, f32[1024,128]{1,0:T(8,128)S(1)}, f32[1024,128]{1,0:T(8,128)S(1)}, f32[1024,1...) custom-call(s32[1]{0:T(128)} %bitcast.1.flip, ...), custom_call_target="tpu_custom_call" | custom-call | flops 8000000000 | bytes 1000000 | tf_op jit(solution)/shard_map/pallas_call | solution.py:388
  14.0 3.6 %shard_map.147 = (f32[1024,128]{1,0:T(8,128)}, f32[520,128]{1,0:T(8,128)S(1)}, f32[520,128]{1,0:T(8,128)S(1)}) custom-call(s32[1]{0:T(128)} %bitcast.1.flip, s32[6,1024]{1,0:T(8,128)S(1)} %bitcast.13, s32[8,128]{1,0:T(8,128)S(1)} %bitcast.16, f32[1024,128]{1,0:T(8,128)S(1)} %copy-done.2, f32[128,128]{1,0:T(8,128)S(1)} %collective-permute-done.left, ...), custom_call_target="tpu_custom_call" | custom-call | flops 4000000000 | bytes 1000000 | tf_op jit(solution)/shard_map/pallas_call | solution.py:388
  17.8 1.5 %collective-permute-done.2 = f32[520,128]{1,0:T(8,128)S(1)} collective-permute-done((f32[520,128]{1,0:T(8,128)S(1)}, f32[520,128]{1,0:T(8,128)S(1)}, u32[]{:S(2)}, u32[]{:S(2)}) %collective-permute-start.2) | collective-permute-done | bytes 266272 | tf_op jit(solution)/shard_map/ppermute | solution.py:407
  19.6 1.8 %collective-permute-start.14 = (f32[256,128]{1,0:T(8,128)S(1)}, f32[256,128]{1,0:T(8,128)S(1)}, u32[]{:S(2)}, u32[]{:S(2)}) collective-permute-start(f32[256,128]{1,0:T(8,128)S(1)} %bitcast.22), channel_id=1, source_target_pairs={{0,2},{1,3},{2,0},{3,1},{4,6},{5,7},{6,4},{7,5},{8,10},{9,11},{10,... | collective-permute-start | bytes 393224 | tf_op jit(solution)/shard_map/ppermute | solution.py:407
  21.4 7.2 %collective-permute-done.3 = f32[520,128]{1,0:T(8,128)S(1)} collective-permute-done((f32[520,128]{1,0:T(8,128)S(1)}, f32[520,128]{1,0:T(8,128)S(1)}, u32[]{:S(2)}, u32[]{:S(2)}) %collective-permute-start.3) | collective-permute-done | bytes 266272 | tf_op jit(solution)/shard_map/ppermute | solution.py:407
  29.1 1.6 %collective-permute-done.14.refs_2_ = f32[256,128]{1,0:T(8,128)S(1)} collective-permute-done((f32[256,128]{1,0:T(8,128)S(1)}, f32[256,128]{1,0:T(8,128)S(1)}, u32[]{:S(2)}, u32[]{:S(2)}) %collective-permute-start.14) | collective-permute-done | bytes 131104 | tf_op jit(solution)/shard_map/ppermute | solution.py:407
  30.7 3.3 %shard_map.150 = (f32[256,128]{1,0:T(8,128)S(1)}, bf16[1024,256]{1,0:T(8,128)(2,1)S(1)}, f32[4,1024,128]{2,1,0:T(8,128)S(1)}, f32[1024,128]{1,0:T(8,128)S(1)}, s...) custom-call(s32[2]{0:T(128)S(1)} %pad_add_fusion.1.flip, ...), custom_call_target="tpu_custom_call" | custom-call | flops 1000000000 | bytes 1000000 | tf_op jit(solution)/shard_map/pallas_call | solution.py:388
  34.0 0.4 shard_map.149
  34.3 0.3 collective-permute-start.5
  34.6 3.6 %collective-permute-start.6 = (f32[128,128]{1,0:T(8,128)S(1)}, f32[128,128]{1,0:T(8,128)S(1)}, u32[]{:S(2)}, u32[]{:S(2)}) collective-permute-start(f32[128,128]{1,0:T(8,128)S(1)} %get-tuple-element.61), channel_id=1, source_target_pairs={{0,12},{4,0},{8,4},{12,8},{1,13},{5,1},{9,5},{13,9},{2,14},{6,2},{... | collective-permute-start | bytes 196616 | tf_op jit(solution)/shard_map/ppermute | solution.py:402
  38.2 2.6 %shard_map.151.before = f32[4,1024,128]{2,1,0:T(8,128)S(1)} custom-call(s32[4,1024]{1,0:T(4,128)S(1)} %bitcast.24, f32[1024,128]{1,0:T(8,128)S(1)} %get-tuple-element.59.nodes, f32[4,1024,128]{2,1,0:T(8,128)S(1)} %get-tuple-element.62.extra, bf16[2,256,256]{2,1,0:T(8,128)(2,1)S(1)} %get-tuple-element.63.weights.first_weights), custom_call_target="tpu_custom_call" | custom-call | flops 3000000000 | bytes 1000000 | tf_op jit(solution)/shard_map/pallas_call | solution.py:388
  41.2 2.6 %shard_map.152 = (f32[1024,128]{1,0:T(8,128)S(1)}, f32[128,128]{1,0:T(8,128)S(1)}, f32[128,128]{1,0:T(8,128)S(1)}) custom-call(s32[1]{0:T(128)} %bitcast.1.flip, s32[4,1024]{1,0:T(4,128)S(1)} %bitcast.25, s32[8,128]{1,0:T(8,128)S(1)} %bitcast.20, f32[1024,128]{1,0:T(8,128)S(1)} %get-tuple-element.59.nodes, f32[128,128]{1,0:T(8,128)S(1)} %collective-permute-done.5.left, ...), custom_call_target="tpu_custom_call" | custom-call | flops 2000000000 | bytes 1000000 | tf_op jit(solution)/shard_map/pallas_call | solution.py:388
  43.7 3.2 %collective-permute-start.7 = (f32[128,128]{1,0:T(8,128)S(1)}, f32[128,128]{1,0:T(8,128)S(1)}, u32[]{:S(2)}, u32[]{:S(2)}) collective-permute-start(f32[128,128]{1,0:T(8,128)S(1)} %get-tuple-element.67.own), channel_id=1, source_target_pairs={{0,12},{4,0},{8,4},{12,8},{1,13},{5,1},{9,5},{13,9},{2,14},{6,2},{... | collective-permute-start | bytes 196616 | tf_op jit(solution)/shard_map/ppermute | solution.py:402
  46.9 0.6 %collective-permute-start.9 = (f32[128,128]{1,0:T(8,128)S(1)}, f32[128,128]{1,0:T(8,128)S(1)}, u32[]{:S(2)}, u32[]{:S(2)}) collective-permute-start(f32[128,128]{1,0:T(8,128)S(1)} %get-tuple-element.67.own), channel_id=1, source_target_pairs={{0,4},{4,8},{8,12},{12,0},{1,5},{5,9},{9,13},{13,1},{2,6},{6,10},{... | collective-permute-start | bytes 196616 | tf_op jit(solution)/shard_map/ppermute | solution.py:402
  47.5 1.8 %shard_map.153.refs_8_ = f32[1024,128]{1,0:T(8,128)S(1)} custom-call(s32[8,128]{1,0:T(8,128)S(1)} %bitcast.18, f32[1024,128]{1,0:T(8,128)S(1)} %get-tuple-element.71.quarter, f32[1024,128]{1,0:T(8,128)} %get-tuple-element.72.fine_new), custom_call_target="tpu_custom_call" | custom-call | flops 1000000000 | bytes 1000000 | tf_op jit(solution)/shard_map/pallas_call | solution.py:388
  49.4 2.6 %collective-permute-done.8.refs_1_ = f32[128,128]{1,0:T(8,128)S(1)} collective-permute-done((f32[128,128]{1,0:T(8,128)S(1)}, f32[128,128]{1,0:T(8,128)S(1)}, u32[]{:S(2)}, u32[]{:S(2)}) %collective-permute-start.8) | collective-permute-done | bytes 65568 | tf_op jit(solution)/shard_map/ppermute | solution.py:402
  52.1 0.9 %collective-permute-done.9.refs_2_ = f32[128,128]{1,0:T(8,128)S(1)} collective-permute-done((f32[128,128]{1,0:T(8,128)S(1)}, f32[128,128]{1,0:T(8,128)S(1)}, u32[]{:S(2)}, u32[]{:S(2)}) %collective-permute-start.9) | collective-permute-done | bytes 65568 | tf_op jit(solution)/shard_map/ppermute | solution.py:402
  53.0 1.2 %shard_map.154 = (f32[4,256,128]{2,1,0:T(8,128)S(1)}, f32[256,128]{1,0:T(8,128)S(1)}) custom-call(s32[3]{0:T(128)S(1)} %pad_add_fusion.place, f32[128,128]{1,0:T(8,128)S(1)} %get-tuple-element.67.own, f32[128,128]{1,0:T(8,128)S(1)} %get-tuple-element.68.partner.own_partner, s16[4,256,128]{2,1,0:T(8,128)(2,1)S(1)} %get-tuple-element.69.columns.refs_6_, ...), custom_call_target="tpu_custom_call" | custom-call | flops 1000000000 | bytes 1000000 | tf_op jit(solution)/shard_map/pallas_call | solution.py:388
  54.2 3.3 %shard_map.155 = f32[1024,128]{1,0:T(8,128)} custom-call(s32[3]{0:T(128)S(1)} %pad_add_fusion.place, f32[128,128]{1,0:T(8,128)S(1)} %get-tuple-element.67.own, f32[128,128]{1,0:T(8,128)S(1)} %get-tuple-element.68.partner.own_partner, f32[128,128]{1,0:T(8,128)S(1)} %collective-permute-done.7.refs_0_, f32[128,128]{1,0:T(8,128)S(1)} %collective-permute-done.8.refs_1_, ...), custom_call_target="tpu_custom_call" | custom-call | flops 2000000000 | bytes 1000000 | tf_op jit(solution)/shard_map/pallas_call | solution.py:388
  (53 shorter events, 1.3 us)
Async XLA Ops:
  2.3 11.6 %collective-permute-start = (f32[128,128]{1,0:T(8,128)S(1)}, f32[128,128]{1,0:T(8,128)S(1)}, u32[]{:S(2)}, u32[]{:S(2)}) collective-permute-start(f32[128,128]{1,0:T(8,128)S(1)} %get-tuple-element.41), channel_id=1, source_target_pairs={{0,1},{1,2},{2,3},{3,4},{4,5},{5,6},{6,7},{7,8},{8,9},{9,10},{10,1... | collective-permute-start | bytes 196616 | tf_op jit(solution)/shard_map/ppermute | solution.py:402
  2.8 11.1 %collective-permute-start.1 = (f32[128,128]{1,0:T(8,128)S(1)}, f32[128,128]{1,0:T(8,128)S(1)}, u32[]{:S(2)}, u32[]{:S(2)}) collective-permute-start(f32[128,128]{1,0:T(8,128)S(1)} %get-tuple-element.42), channel_id=1, source_target_pairs={{0,15},{1,0},{2,1},{3,2},{4,3},{5,4},{6,5},{7,6},{8,7},{9,8},{10,9... | collective-permute-start | bytes 196616 | tf_op jit(solution)/shard_map/ppermute | solution.py:402
  8.8 5.2 %copy-start.5 = (f32[3,128,128]{2,1,0:T(8,128)S(1)}, f32[3,128,128]{2,1,0:T(8,128)}, u32[]{:S(2)}) copy-start(f32[3,128,128]{2,1,0:T(8,128)} %node_out.1) | copy-start | bytes 589828
  8.8 5.2 %copy-start.6 = (s32[1024,6]{0,1:T(8,128)S(1)}, s32[1024,6]{0,1:T(8,128)}, u32[]{:S(2)}) copy-start(s32[1024,6]{0,1:T(8,128)} %param.17) | copy-start | bytes 73732
  14.0 5.4 %copy-start.13 = (f32[64,4,128]{2,1,0:T(4,128)S(1)}, f32[64,4,128]{2,1,0:T(4,128)}, u32[]{:S(2)}) copy-start(f32[64,4,128]{2,1,0:T(4,128)} %param.24) | copy-start | bytes 393220
  17.7 13.0 %copy-start.1 = (f32[1024,4,128]{2,1,0:T(4,128)S(1)}, f32[1024,4,128]{2,1,0:T(4,128)}, u32[]{:S(2)}) copy-start(f32[1024,4,128]{2,1,0:T(4,128)} %param.20) | copy-start | bytes 6291460
  17.7 13.0 %copy-start.7 = (s32[1024,4]{0,1:T(4,128)S(1)}, s32[1024,4]{0,1:T(4,128)}, u32[]{:S(2)}) copy-start(s32[1024,4]{0,1:T(4,128)} %param.25) | copy-start | bytes 49156
  17.7 13.0 %copy-start.9 = (s32[1024]{0:T(1024)S(1)}, s32[1024]{0:T(1024)}, u32[]{:S(2)}) copy-start(s32[1024]{0:T(1024)} %param.23) | copy-start | bytes 12292
  17.7 1.6 %collective-permute-start.2 = (f32[520,128]{1,0:T(8,128)S(1)}, f32[520,128]{1,0:T(8,128)S(1)}, u32[]{:S(2)}, u32[]{:S(2)}) collective-permute-start(f32[520,128]{1,0:T(8,128)S(1)} %get-tuple-element.58), channel_id=1, source_target_pairs={{0,1},{1,0},{2,3},{3,2},{4,5},{5,4},{6,7},{7,6},{8,9},{9,8},{10,11... | collective-permute-start | bytes 798728 | tf_op jit(solution)/shard_map/ppermute | solution.py:407
  19.3 9.3 %collective-permute-start.3 = (f32[520,128]{1,0:T(8,128)S(1)}, f32[520,128]{1,0:T(8,128)S(1)}, u32[]{:S(2)}, u32[]{:S(2)}) collective-permute-start(f32[520,128]{1,0:T(8,128)S(1)} %add.11._), channel_id=1, source_target_pairs={{0,2},{1,3},{2,0},{3,1},{4,6},{5,7},{6,4},{7,5},{8,10},{9,11},{10,... | collective-permute-start | bytes 798728 | tf_op jit(solution)/shard_map/ppermute | solution.py:407
  19.4 33.5 %collective-permute-start.13 = (f32[256,128]{1,0:T(8,128)S(1)}, f32[256,128]{1,0:T(8,128)S(1)}, u32[]{:S(2)}, u32[]{:S(2)}) collective-permute-start(f32[256,128]{1,0:T(8,128)S(1)} %bitcast.21), channel_id=1, source_target_pairs={{0,1},{1,0},{2,3},{3,2},{4,5},{5,4},{6,7},{7,6},{8,9},{9,8},{10,11... | collective-permute-start | bytes 393224 | tf_op jit(solution)/shard_map/ppermute | solution.py:407
  19.6 11.0 %collective-permute-start.14 = (f32[256,128]{1,0:T(8,128)S(1)}, f32[256,128]{1,0:T(8,128)S(1)}, u32[]{:S(2)}, u32[]{:S(2)}) collective-permute-start(f32[256,128]{1,0:T(8,128)S(1)} %bitcast.22), channel_id=1, source_target_pairs={{0,2},{1,3},{2,0},{3,1},{4,6},{5,7},{6,4},{7,5},{8,10},{9,11},{10,... | collective-permute-start | bytes 393224 | tf_op jit(solution)/shard_map/ppermute | solution.py:407
  28.7 5.3 %copy-start.10 = (s32[2,128]{1,0:T(2,128)S(1)}, s32[2,128]{1,0:T(2,128)}, u32[]{:S(2)}) copy-start(s32[2,128]{1,0:T(2,128)} %lists.3) | copy-start | bytes 3076
  28.9 5.1 %collective-permute-start.4 = (f32[512,128]{1,0:T(8,128)S(1)}, f32[512,128]{1,0:T(8,128)S(1)}, u32[]{:S(2)}, u32[]{:S(2)}) collective-permute-start(f32[512,128]{1,0:T(8,128)S(1)} %shard_map.148.mine), channel_id=1, source_target_pairs={{0,1},{1,0},{2,3},{3,2},{4,5},{5,4},{6,7},{7,6},{8,9},{9,8},{10,11... | collective-permute-start | bytes 786440 | tf_op jit(solution)/shard_map/ppermute | solution.py:407
  30.7 22.3 %collective-permute-start.15 = (f32[256,128]{1,0:T(8,128)S(1)}, f32[256,128]{1,0:T(8,128)S(1)}, u32[]{:S(2)}, u32[]{:S(2)}) collective-permute-start(f32[256,128]{1,0:T(8,128)S(1)} %collective-permute-done.14.refs_2_), channel_id=1, source_target_pairs={{0,1},{1,0},{2,3},{3,2},{4,5},{5,4},{6,7},{7,6},{8,9},{9,8},{10,11... | collective-permute-start | bytes 393224 | tf_op jit(solution)/shard_map/ppermute | solution.py:407
  30.7 7.5 %copy-start.14 = (s32[1024,4]{0,1:T(4,128)S(1)}, s32[1024,4]{0,1:T(4,128)}, u32[]{:S(2)}) copy-start(s32[1024,4]{0,1:T(4,128)} %param.21) | copy-start | bytes 49156
  34.3 6.8 %collective-permute-start.5 = (f32[128,128]{1,0:T(8,128)S(1)}, f32[128,128]{1,0:T(8,128)S(1)}, u32[]{:S(2)}, u32[]{:S(2)}) collective-permute-start(f32[128,128]{1,0:T(8,128)S(1)} %get-tuple-element.60), channel_id=1, source_target_pairs={{0,4},{4,8},{8,12},{12,0},{1,5},{5,9},{9,13},{13,1},{2,6},{6,10},{... | collective-permute-start | bytes 196616 | tf_op jit(solution)/shard_map/ppermute | solution.py:402
  34.6 6.5 %collective-permute-start.6 = (f32[128,128]{1,0:T(8,128)S(1)}, f32[128,128]{1,0:T(8,128)S(1)}, u32[]{:S(2)}, u32[]{:S(2)}) collective-permute-start(f32[128,128]{1,0:T(8,128)S(1)} %get-tuple-element.61), channel_id=1, source_target_pairs={{0,12},{4,0},{8,4},{12,8},{1,13},{5,1},{9,5},{13,9},{2,14},{6,2},{... | collective-permute-start | bytes 196616 | tf_op jit(solution)/shard_map/ppermute | solution.py:402
  43.7 5.6 %collective-permute-start.7 = (f32[128,128]{1,0:T(8,128)S(1)}, f32[128,128]{1,0:T(8,128)S(1)}, u32[]{:S(2)}, u32[]{:S(2)}) collective-permute-start(f32[128,128]{1,0:T(8,128)S(1)} %get-tuple-element.67.own), channel_id=1, source_target_pairs={{0,12},{4,0},{8,4},{12,8},{1,13},{5,1},{9,5},{13,9},{2,14},{6,2},{... | collective-permute-start | bytes 196616 | tf_op jit(solution)/shard_map/ppermute | solution.py:402
  46.9 5.2 %collective-permute-start.8 = (f32[128,128]{1,0:T(8,128)S(1)}, f32[128,128]{1,0:T(8,128)S(1)}, u32[]{:S(2)}, u32[]{:S(2)}) collective-permute-start(f32[128,128]{1,0:T(8,128)S(1)} %get-tuple-element.67.own), channel_id=1, source_target_pairs={{0,8},{4,12},{8,0},{12,4},{1,9},{5,13},{9,1},{13,5},{2,10},{6,14},... | collective-permute-start | bytes 196616 | tf_op jit(solution)/shard_map/ppermute | solution.py:402
  46.9 6.1 %collective-permute-start.9 = (f32[128,128]{1,0:T(8,128)S(1)}, f32[128,128]{1,0:T(8,128)S(1)}, u32[]{:S(2)}, u32[]{:S(2)}) collective-permute-start(f32[128,128]{1,0:T(8,128)S(1)} %get-tuple-element.67.own), channel_id=1, source_target_pairs={{0,4},{4,8},{8,12},{12,0},{1,5},{5,9},{9,13},{13,1},{2,6},{6,10},{... | collective-permute-start | bytes 196616 | tf_op jit(solution)/shard_map/ppermute | solution.py:402
  49.4 4.8 %collective-permute-start.10 = (f32[128,128]{1,0:T(8,128)S(1)}, f32[128,128]{1,0:T(8,128)S(1)}, u32[]{:S(2)}, u32[]{:S(2)}) collective-permute-start(f32[128,128]{1,0:T(8,128)S(1)} %collective-permute-done.7.refs_0_), channel_id=1, source_target_pairs={{0,1},{1,0},{2,3},{3,2},{4,5},{5,4},{6,7},{7,6},{8,9},{9,8},{10,11... | collective-permute-start | bytes 196616 | tf_op jit(solution)/shard_map/ppermute | solution.py:407
  52.1 2.1 %collective-permute-start.11 = (f32[128,128]{1,0:T(8,128)S(1)}, f32[128,128]{1,0:T(8,128)S(1)}, u32[]{:S(2)}, u32[]{:S(2)}) collective-permute-start(f32[128,128]{1,0:T(8,128)S(1)} %collective-permute-done.8.refs_1_), channel_id=1, source_target_pairs={{0,1},{1,0},{2,3},{3,2},{4,5},{5,4},{6,7},{7,6},{8,9},{9,8},{10,11... | collective-permute-start | bytes 196616 | tf_op jit(solution)/shard_map/ppermute | solution.py:407
  53.0 1.3 %collective-permute-start.12 = (f32[128,128]{1,0:T(8,128)S(1)}, f32[128,128]{1,0:T(8,128)S(1)}, u32[]{:S(2)}, u32[]{:S(2)}) collective-permute-start(f32[128,128]{1,0:T(8,128)S(1)} %collective-permute-done.9.refs_2_), channel_id=1, source_target_pairs={{0,1},{1,0},{2,3},{3,2},{4,5},{5,4},{6,7},{7,6},{8,9},{9,8},{10,11... | collective-permute-start | bytes 196616 | tf_op jit(solution)/shard_map/ppermute | solution.py:407
  (7 other events, 27.7 us)

commit v3 on v2

--- a/solution.py
+++ b/solution.py
@@ -289,7 +289,7 @@
 
 
 def quarter_second_kernel(
-    flip, senders, pool, nodes, left, right, before, edge_sum, share, first_weights, weights, new, own, partner, beyond,
+    flip, senders, pool, nodes, left, right, before, edge_sum, share, first_weights, weights, new, own, beyond,
 ):
     degree, rows, _ = before.shape
     margin = left.shape[0]
@@ -305,13 +305,16 @@
     target = rotated(target, flip[0], part)
     split = side(updated)
     first = pl.multiple_of(flip[0] * part, part)
+    own[...] = folded(times(members(target, part), split)) * share[pl.ds(first, part), :]
+
+
+def base_kernel(flip, pool, quarter_pool, quarter, share, fine_new, out, partner):
+    both = side(quarter[...])
+    part = partner.shape[0]
+    target = jnp.concatenate([quarter_pool[j : j + 1, :] for j in range(quarter_pool.shape[0])], axis=1)
+    target = rotated(target, flip[0], part) - part
     second = pl.multiple_of((1 - flip[0]) * part, part)
-    own[...] = folded(times(members(target, part), split)) * share[pl.ds(first, part), :]
-    partner[...] = folded(times(members(target - part, part), split)) * share[pl.ds(second, part), :]
-
-
-def base_kernel(pool, quarter, fine_new, out):
-    both = side(quarter[...])
+    partner[...] = folded(times(members(target, part), both)) * share[pl.ds(second, part), :]
     column = jnp.concatenate([down(pool[r : r + 1, :]) for r in range(pool.shape[0])], axis=0)
     out[...] = fine_new[...] + folded(times(picks(column, both.shape[0]), both))
 
@@ -420,7 +423,7 @@
     total = coarse_senders.shape[0]
     block = total // n_patch
     part, c_part = q_rows // 2, block // 2
-    tile = min(512, q_rows)
+    tile = min(1024, q_rows)
     lines = part // LANES
     height = -(-lines // 8) * 8
     core = sub % 2
@@ -541,7 +544,7 @@
         (quarter_senders, quarter_nodes, quarter_before, quarter_weights),
         shaped(q_degree, q_rows, w), whole(q_degree, q_rows, w), [pltpu.VMEM((q_rows, 2 * w), half)], 20, 3 * 10**9,
     )
-    quarter_new, own, own_partner = run(
+    quarter_new, own = run(
         quarter_second_kernel, (1,), (flip,),
         [
             whole(q_degree, q_rows), whole(*quarter_pool_rows.shape), whole(q_rows, w), whole(q_margin, w),
@@ -550,16 +553,17 @@
         ],
         (quarter_senders, quarter_pool_rows, quarter_nodes, left, right, quarter_first, quarter_sum, coarse_share,
          quarter_weights, quarter_later),
-        (shaped(q_rows, w), shaped(c_part, w), shaped(c_part, w)),
-        [whole(q_rows, w), whole(c_part, w), whole(c_part, w)],
+        (shaped(q_rows, w), shaped(c_part, w)), [whole(q_rows, w), whole(c_part, w)],
         [pltpu.VMEM((2 * q_margin, 2 * w), half)], 20, 2 * 10**9,
     )
 
     pieces = [own] + [passed(own, "patch", -j) for j in range(1, n_patch)]
-    partner = [own_partner] + [swapped(pieces[j], "sub", 1) for j in range(1, n_patch)]
-    base = run(
-        base_kernel, (1,), (), [whole(*pool_rows.shape), whole(q_rows, w), whole(rows, w)],
-        (pool_rows, quarter_new, hbm(fine_new)), shaped(rows, w), whole(rows, w), [], 16, 10**9,
+    partner = [swapped(pieces[j], "sub", 1) for j in range(1, n_patch)]
+    base, own_partner = run(
+        base_kernel, (1,), (flip,),
+        [whole(*pool_rows.shape), whole(*quarter_pool_rows.shape), whole(q_rows, w), whole(block, w), whole(rows, w)],
+        (pool_rows, quarter_pool_rows, quarter_new, coarse_share, hbm(fine_new)), (shaped(rows, w), shaped(c_part, w)),
+        [whole(rows, w), whole(c_part, w)], [], 16, 10**9,
     )
     place = jnp.stack([patch, core, sub])
     before, edge_sum = run(
@@ -582,7 +586,7 @@
             *[whole(c_part, w)] * (2 * n_patch), whole(c_degree, block, w), whole(rows, block), whole(rows, w),
             whole(c_degree, block, w), whole(block, w), whole(*mats(3)), whole(*mats(4)),
         ],
-        (own, own_partner, *pieces[1:], *partner[1:], coarse_columns, chosen, base, before, edge_sum, coarse_weights,
+        (own, own_partner, *pieces[1:], *partner, coarse_columns, chosen, base, before, edge_sum, coarse_weights,
          coarse_later),
         shaped(rows, w), in_hbm,
         [

time: 58 us -> 57.8 us (level)
  no operation moved by 1% of the time
where the time goes in v3:
time: 57.8 us; the launch traced here: 57.5 us
  Pallas kernels  25.3 us (44%)
  starting transfers between devices  15.4 us (27%)
  waiting for transfers between devices  14.1 us (24%)
  local copies, waits for them, and re-layouts  1.9 us (3%)
    pallas_call x11, Pallas kernels, run(): pl.pallas_call(kernel, out_shape=outs, grid_spec=pltpu.PrefetchScalarGrid...  25.3 us
    ppermute x7, starting transfers between devices, passed(): lax.ppermute(value, axis, [(s, (s + steps) % count) for s in range(count)])  13.1 us
    ppermute x9, waiting for transfers between devices, swapped(): return lax.ppermute(value, axis, [(s, s ^ bit) for s in range(count)])  10.4 us
    ppermute x7, waiting for transfers between devices, passed(): lax.ppermute(value, axis, [(s, (s + steps) % count) for s in range(count)])  3.74 us
    ppermute x9, starting transfers between devices, swapped(): return lax.ppermute(value, axis, [(s, s ^ bit) for s in range(count)])  2.3 us
    unnamed x30, local copies, waits for them, and re-layouts  1.9 us
  transfers between devices with their start and end apart: 16, of which 7 were waited for; matrix products, arithmetic and copies ran while one was open for 0% of the time, Pallas kernels for 29%

profile of v3, /device:TPU:0, one launch (start us, length us, event | category | flops | bytes accessed | tf_op | source)
XLA Modules:
  0.0 57.5 jit_solution(4308850391586404505)
XLA Ops:
  0.0 1.5 %shard_map.145 = (f32[128,128]{1,0:T(8,128)S(1)}, f32[128,128]{1,0:T(8,128)S(1)}, f32[1024,128]{1,0:T(8,128)S(1)}, s32[6,1024]{1,0:T(8,128)S(1)}, s32[8,128]{1,0...) custom-call(s32[2,128]{1,0:T(2,128)} %lists.2, ...), custom_call_target="tpu_custom_call" | custom-call | flops 100000000 | bytes 1000000 | tf_op jit(solution)/shard_map/pallas_call | solution.py:391
  1.5 0.8 %copy-done.11 = f32[1024,128]{1,0:T(8,128)} copy-done((f32[1024,128]{1,0:T(8,128)}, f32[1024,128]{1,0:T(8,128)S(1)}, u32[]{:S(2)}) %copy-start.11) | copy-done | bytes 524312
  2.3 0.5 collective-permute-start
  2.8 5.0 %collective-permute-start.1 = (f32[128,128]{1,0:T(8,128)S(1)}, f32[128,128]{1,0:T(8,128)S(1)}, u32[]{:S(2)}, u32[]{:S(2)}) collective-permute-start(f32[128,128]{1,0:T(8,128)S(1)} %get-tuple-element.43), channel_id=1, source_target_pairs={{0,15},{1,0},{2,1},{3,2},{4,3},{5,4},{6,5},{7,6},{8,7},{9,8},{10,9... | collective-permute-start | bytes 196616 | tf_op jit(solution)/shard_map/ppermute | solution.py:405
  7.8 1.0 %copy-done.12 = f32[1024,128]{1,0:T(8,128)S(1)} copy-done((f32[1024,128]{1,0:T(8,128)S(1)}, f32[1024,128]{1,0:T(8,128)}, u32[]{:S(2)}) %copy-start.12) | copy-done | bytes 524312
  8.9 5.1 %shard_map.146 = (f32[1024,128]{1,0:T(8,128)S(1)}, f32[1024,128]{1,0:T(8,128)S(1)}, f32[1024,128]{1,0:T(8,128)S(1)}, f32[1024,128]{1,0:T(8,128)S(1)}, f32[1024,1...) custom-call(s32[1]{0:T(128)} %bitcast.1.flip, ...), custom_call_target="tpu_custom_call" | custom-call | flops 8000000000 | bytes 1000000 | tf_op jit(solution)/shard_map/pallas_call | solution.py:391
  14.0 3.6 %shard_map.147 = (f32[1024,128]{1,0:T(8,128)}, f32[520,128]{1,0:T(8,128)S(1)}, f32[520,128]{1,0:T(8,128)S(1)}) custom-call(s32[1]{0:T(128)} %bitcast.1.flip, s32[6,1024]{1,0:T(8,128)S(1)} %bitcast.13, s32[8,128]{1,0:T(8,128)S(1)} %bitcast.16, f32[1024,128]{1,0:T(8,128)S(1)} %copy-done.2, f32[128,128]{1,0:T(8,128)S(1)} %collective-permute-done.left, ...), custom_call_target="tpu_custom_call" | custom-call | flops 4000000000 | bytes 1000000 | tf_op jit(solution)/shard_map/pallas_call | solution.py:391
  17.8 1.5 %collective-permute-done.2 = f32[520,128]{1,0:T(8,128)S(1)} collective-permute-done((f32[520,128]{1,0:T(8,128)S(1)}, f32[520,128]{1,0:T(8,128)S(1)}, u32[]{:S(2)}, u32[]{:S(2)}) %collective-permute-start.2) | collective-permute-done | bytes 266272 | tf_op jit(solution)/shard_map/ppermute | solution.py:410
  19.6 1.8 %collective-permute-start.14 = (f32[256,128]{1,0:T(8,128)S(1)}, f32[256,128]{1,0:T(8,128)S(1)}, u32[]{:S(2)}, u32[]{:S(2)}) collective-permute-start(f32[256,128]{1,0:T(8,128)S(1)} %bitcast.23), channel_id=1, source_target_pairs={{0,2},{1,3},{2,0},{3,1},{4,6},{5,7},{6,4},{7,5},{8,10},{9,11},{10,... | collective-permute-start | bytes 393224 | tf_op jit(solution)/shard_map/ppermute | solution.py:410
  21.4 7.2 %collective-permute-done.3 = f32[520,128]{1,0:T(8,128)S(1)} collective-permute-done((f32[520,128]{1,0:T(8,128)S(1)}, f32[520,128]{1,0:T(8,128)S(1)}, u32[]{:S(2)}, u32[]{:S(2)}) %collective-permute-start.3) | collective-permute-done | bytes 266272 | tf_op jit(solution)/shard_map/ppermute | solution.py:410
  29.1 1.6 %collective-permute-done.14.refs_2_ = f32[256,128]{1,0:T(8,128)S(1)} collective-permute-done((f32[256,128]{1,0:T(8,128)S(1)}, f32[256,128]{1,0:T(8,128)S(1)}, u32[]{:S(2)}, u32[]{:S(2)}) %collective-permute-start.14) | collective-permute-done | bytes 131104 | tf_op jit(solution)/shard_map/ppermute | solution.py:410
  30.7 3.3 %shard_map.150 = (f32[256,128]{1,0:T(8,128)S(1)}, bf16[1024,256]{1,0:T(8,128)(2,1)S(1)}, f32[4,1024,128]{2,1,0:T(8,128)S(1)}, f32[1024,128]{1,0:T(8,128)S(1)}, s...) custom-call(s32[2]{0:T(128)S(1)} %pad_add_fusion.1.flip, ...), custom_call_target="tpu_custom_call" | custom-call | flops 1000000000 | bytes 1000000 | tf_op jit(solution)/shard_map/pallas_call | solution.py:391
  34.0 0.4 shard_map.149
  34.3 0.3 collective-permute-start.5
  34.6 3.6 %collective-permute-start.6 = (f32[128,128]{1,0:T(8,128)S(1)}, f32[128,128]{1,0:T(8,128)S(1)}, u32[]{:S(2)}, u32[]{:S(2)}) collective-permute-start(f32[128,128]{1,0:T(8,128)S(1)} %get-tuple-element.62), channel_id=1, source_target_pairs={{0,12},{4,0},{8,4},{12,8},{1,13},{5,1},{9,5},{13,9},{2,14},{6,2},{... | collective-permute-start | bytes 196616 | tf_op jit(solution)/shard_map/ppermute | solution.py:405
  38.2 2.7 %shard_map.151.before = f32[4,1024,128]{2,1,0:T(8,128)S(1)} custom-call(s32[4,1024]{1,0:T(4,128)S(1)} %bitcast.25, f32[1024,128]{1,0:T(8,128)S(1)} %get-tuple-element.60.nodes, f32[4,1024,128]{2,1,0:T(8,128)S(1)} %get-tuple-element.63.extra, bf16[2,256,256]{2,1,0:T(8,128)(2,1)S(1)} %get-tuple-element.64.weights.first_weights), custom_call_target="tpu_custom_call" | custom-call | flops 3000000000 | bytes 1000000 | tf_op jit(solution)/shard_map/pallas_call | solution.py:391
  41.2 2.4 %shard_map.152 = (f32[1024,128]{1,0:T(8,128)S(1)}, f32[128,128]{1,0:T(8,128)S(1)}) custom-call(s32[1]{0:T(128)} %bitcast.1.flip, s32[4,1024]{1,0:T(4,128)S(1)} %bitcast.26, s32[8,128]{1,0:T(8,128)S(1)} %bitcast.20, f32[1024,128]{1,0:T(8,128)S(1)} %get-tuple-element.60.nodes, f32[128,128]{1,0:T(8,128)S(1)} %collective-permute-done.5.left, ...), custom_call_target="tpu_custom_call" | custom-call | flops 2000000000 | bytes 1000000 | tf_op jit(solution)/shard_map/pallas_call | solution.py:391
  43.5 3.2 %collective-permute-start.7 = (f32[128,128]{1,0:T(8,128)S(1)}, f32[128,128]{1,0:T(8,128)S(1)}, u32[]{:S(2)}, u32[]{:S(2)}) collective-permute-start(f32[128,128]{1,0:T(8,128)S(1)} %get-tuple-element.68.own), channel_id=1, source_target_pairs={{0,12},{4,0},{8,4},{12,8},{1,13},{5,1},{9,5},{13,9},{2,14},{6,2},{... | collective-permute-start | bytes 196616 | tf_op jit(solution)/shard_map/ppermute | solution.py:405
  46.7 0.6 %collective-permute-start.9 = (f32[128,128]{1,0:T(8,128)S(1)}, f32[128,128]{1,0:T(8,128)S(1)}, u32[]{:S(2)}, u32[]{:S(2)}) collective-permute-start(f32[128,128]{1,0:T(8,128)S(1)} %get-tuple-element.68.own), channel_id=1, source_target_pairs={{0,4},{4,8},{8,12},{12,0},{1,5},{5,9},{9,13},{13,1},{2,6},{6,10},{... | collective-permute-start | bytes 196616 | tf_op jit(solution)/shard_map/ppermute | solution.py:405
  47.4 1.9 %shard_map.153 = (f32[1024,128]{1,0:T(8,128)S(1)}, f32[128,128]{1,0:T(8,128)S(1)}) custom-call(s32[1]{0:T(128)} %bitcast.1.flip, s32[8,128]{1,0:T(8,128)S(1)} %bitcast.18, s32[8,128]{1,0:T(8,128)S(1)} %bitcast.21, f32[1024,128]{1,0:T(8,128)S(1)} %get-tuple-element.69.quarter, f32[256,128]{1,0:T(8,128)S(1)} %get-tuple-element.66.share, ...), custom_call_target="tpu_custom_call" | custom-call | flops 1000000000 | bytes 1000000 | tf_op jit(solution)/shard_map/pallas_call | solution.py:391
  49.3 2.6 %collective-permute-done.8.refs_1_ = f32[128,128]{1,0:T(8,128)S(1)} collective-permute-done((f32[128,128]{1,0:T(8,128)S(1)}, f32[128,128]{1,0:T(8,128)S(1)}, u32[]{:S(2)}, u32[]{:S(2)}) %collective-permute-start.8) | collective-permute-done | bytes 65568 | tf_op jit(solution)/shard_map/ppermute | solution.py:405
  51.9 0.9 %collective-permute-done.9.refs_2_ = f32[128,128]{1,0:T(8,128)S(1)} collective-permute-done((f32[128,128]{1,0:T(8,128)S(1)}, f32[128,128]{1,0:T(8,128)S(1)}, u32[]{:S(2)}, u32[]{:S(2)}) %collective-permute-start.9) | collective-permute-done | bytes 65568 | tf_op jit(solution)/shard_map/ppermute | solution.py:405
  52.8 1.2 %shard_map.154 = (f32[4,256,128]{2,1,0:T(8,128)S(1)}, f32[256,128]{1,0:T(8,128)S(1)}) custom-call(s32[3]{0:T(128)S(1)} %pad_add_fusion.place, f32[128,128]{1,0:T(8,128)S(1)} %get-tuple-element.68.own, f32[128,128]{1,0:T(8,128)S(1)} %get-tuple-element.71.partner.own_partner, s16[4,256,128]{2,1,0:T(8,128)(2,1)S(1)} %get-tuple-element.72.columns.refs_6_, ...), custom_call_target="tpu_custom_call" | custom-call | flops 1000000000 | bytes 1000000 | tf_op jit(solution)/shard_map/pallas_call | solution.py:391
  54.0 3.3 %shard_map.155 = f32[1024,128]{1,0:T(8,128)} custom-call(s32[3]{0:T(128)S(1)} %pad_add_fusion.place, f32[128,128]{1,0:T(8,128)S(1)} %get-tuple-element.68.own, f32[128,128]{1,0:T(8,128)S(1)} %get-tuple-element.71.partner.own_partner, f32[128,128]{1,0:T(8,128)S(1)} %collective-permute-done.7.refs_0_, f32[128,128]{1,0:T(8,128)S(1)} %collective-permute-done.8.refs_1_, ...), custom_call_target="tpu_custom_call" | custom-call | flops 2000000000 | bytes 1000000 | tf_op jit(solution)/shard_map/pallas_call | solution.py:391
  (53 shorter events, 1.3 us)
Async XLA Ops:
  2.3 11.6 %collective-permute-start = (f32[128,128]{1,0:T(8,128)S(1)}, f32[128,128]{1,0:T(8,128)S(1)}, u32[]{:S(2)}, u32[]{:S(2)}) collective-permute-start(f32[128,128]{1,0:T(8,128)S(1)} %get-tuple-element.42), channel_id=1, source_target_pairs={{0,1},{1,2},{2,3},{3,4},{4,5},{5,6},{6,7},{7,8},{8,9},{9,10},{10,1... | collective-permute-start | bytes 196616 | tf_op jit(solution)/shard_map/ppermute | solution.py:405
  2.8 11.1 %collective-permute-start.1 = (f32[128,128]{1,0:T(8,128)S(1)}, f32[128,128]{1,0:T(8,128)S(1)}, u32[]{:S(2)}, u32[]{:S(2)}) collective-permute-start(f32[128,128]{1,0:T(8,128)S(1)} %get-tuple-element.43), channel_id=1, source_target_pairs={{0,15},{1,0},{2,1},{3,2},{4,3},{5,4},{6,5},{7,6},{8,7},{9,8},{10,9... | collective-permute-start | bytes 196616 | tf_op jit(solution)/shard_map/ppermute | solution.py:405
  8.8 5.2 %copy-start.5 = (f32[3,128,128]{2,1,0:T(8,128)S(1)}, f32[3,128,128]{2,1,0:T(8,128)}, u32[]{:S(2)}) copy-start(f32[3,128,128]{2,1,0:T(8,128)} %node_out.1) | copy-start | bytes 589828
  8.8 5.2 %copy-start.6 = (s32[1024,6]{0,1:T(8,128)S(1)}, s32[1024,6]{0,1:T(8,128)}, u32[]{:S(2)}) copy-start(s32[1024,6]{0,1:T(8,128)} %param.17) | copy-start | bytes 73732
  14.0 5.4 %copy-start.13 = (f32[64,4,128]{2,1,0:T(4,128)S(1)}, f32[64,4,128]{2,1,0:T(4,128)}, u32[]{:S(2)}) copy-start(f32[64,4,128]{2,1,0:T(4,128)} %param.24) | copy-start | bytes 393220
  17.7 13.0 %copy-start.1 = (f32[1024,4,128]{2,1,0:T(4,128)S(1)}, f32[1024,4,128]{2,1,0:T(4,128)}, u32[]{:S(2)}) copy-start(f32[1024,4,128]{2,1,0:T(4,128)} %param.20) | copy-start | bytes 6291460
  17.7 13.0 %copy-start.7 = (s32[1024,4]{0,1:T(4,128)S(1)}, s32[1024,4]{0,1:T(4,128)}, u32[]{:S(2)}) copy-start(s32[1024,4]{0,1:T(4,128)} %param.25) | copy-start | bytes 49156
  17.7 13.0 %copy-start.9 = (s32[1024]{0:T(1024)S(1)}, s32[1024]{0:T(1024)}, u32[]{:S(2)}) copy-start(s32[1024]{0:T(1024)} %param.23) | copy-start | bytes 12292
  17.7 1.6 %collective-permute-start.2 = (f32[520,128]{1,0:T(8,128)S(1)}, f32[520,128]{1,0:T(8,128)S(1)}, u32[]{:S(2)}, u32[]{:S(2)}) collective-permute-start(f32[520,128]{1,0:T(8,128)S(1)} %get-tuple-element.59), channel_id=1, source_target_pairs={{0,1},{1,0},{2,3},{3,2},{4,5},{5,4},{6,7},{7,6},{8,9},{9,8},{10,11... | collective-permute-start | bytes 798728 | tf_op jit(solution)/shard_map/ppermute | solution.py:410
  19.3 9.3 %collective-permute-start.3 = (f32[520,128]{1,0:T(8,128)S(1)}, f32[520,128]{1,0:T(8,128)S(1)}, u32[]{:S(2)}, u32[]{:S(2)}) collective-permute-start(f32[520,128]{1,0:T(8,128)S(1)} %add.11._), channel_id=1, source_target_pairs={{0,2},{1,3},{2,0},{3,1},{4,6},{5,7},{6,4},{7,5},{8,10},{9,11},{10,... | collective-permute-start | bytes 798728 | tf_op jit(solution)/shard_map/ppermute | solution.py:410
  19.4 33.4 %collective-permute-start.13 = (f32[256,128]{1,0:T(8,128)S(1)}, f32[256,128]{1,0:T(8,128)S(1)}, u32[]{:S(2)}, u32[]{:S(2)}) collective-permute-start(f32[256,128]{1,0:T(8,128)S(1)} %bitcast.22), channel_id=1, source_target_pairs={{0,1},{1,0},{2,3},{3,2},{4,5},{5,4},{6,7},{7,6},{8,9},{9,8},{10,11... | collective-permute-start | bytes 393224 | tf_op jit(solution)/shard_map/ppermute | solution.py:410
  19.6 11.0 %collective-permute-start.14 = (f32[256,128]{1,0:T(8,128)S(1)}, f32[256,128]{1,0:T(8,128)S(1)}, u32[]{:S(2)}, u32[]{:S(2)}) collective-permute-start(f32[256,128]{1,0:T(8,128)S(1)} %bitcast.23), channel_id=1, source_target_pairs={{0,2},{1,3},{2,0},{3,1},{4,6},{5,7},{6,4},{7,5},{8,10},{9,11},{10,... | collective-permute-start | bytes 393224 | tf_op jit(solution)/shard_map/ppermute | solution.py:410
  28.7 5.3 %copy-start.10 = (s32[2,128]{1,0:T(2,128)S(1)}, s32[2,128]{1,0:T(2,128)}, u32[]{:S(2)}) copy-start(s32[2,128]{1,0:T(2,128)} %lists.3) | copy-start | bytes 3076
  28.9 5.1 %collective-permute-start.4 = (f32[512,128]{1,0:T(8,128)S(1)}, f32[512,128]{1,0:T(8,128)S(1)}, u32[]{:S(2)}, u32[]{:S(2)}) collective-permute-start(f32[512,128]{1,0:T(8,128)S(1)} %shard_map.148.mine), channel_id=1, source_target_pairs={{0,1},{1,0},{2,3},{3,2},{4,5},{5,4},{6,7},{7,6},{8,9},{9,8},{10,11... | collective-permute-start | bytes 786440 | tf_op jit(solution)/shard_map/ppermute | solution.py:410
  30.7 22.1 %collective-permute-start.15 = (f32[256,128]{1,0:T(8,128)S(1)}, f32[256,128]{1,0:T(8,128)S(1)}, u32[]{:S(2)}, u32[]{:S(2)}) collective-permute-start(f32[256,128]{1,0:T(8,128)S(1)} %collective-permute-done.14.refs_2_), channel_id=1, source_target_pairs={{0,1},{1,0},{2,3},{3,2},{4,5},{5,4},{6,7},{7,6},{8,9},{9,8},{10,11... | collective-permute-start | bytes 393224 | tf_op jit(solution)/shard_map/ppermute | solution.py:410
  30.7 7.5 %copy-start.14 = (s32[1024,4]{0,1:T(4,128)S(1)}, s32[1024,4]{0,1:T(4,128)}, u32[]{:S(2)}) copy-start(s32[1024,4]{0,1:T(4,128)} %param.21) | copy-start | bytes 49156
  34.3 6.8 %collective-permute-start.5 = (f32[128,128]{1,0:T(8,128)S(1)}, f32[128,128]{1,0:T(8,128)S(1)}, u32[]{:S(2)}, u32[]{:S(2)}) collective-permute-start(f32[128,128]{1,0:T(8,128)S(1)} %get-tuple-element.61), channel_id=1, source_target_pairs={{0,4},{4,8},{8,12},{12,0},{1,5},{5,9},{9,13},{13,1},{2,6},{6,10},{... | collective-permute-start | bytes 196616 | tf_op jit(solution)/shard_map/ppermute | solution.py:405
  34.6 6.5 %collective-permute-start.6 = (f32[128,128]{1,0:T(8,128)S(1)}, f32[128,128]{1,0:T(8,128)S(1)}, u32[]{:S(2)}, u32[]{:S(2)}) collective-permute-start(f32[128,128]{1,0:T(8,128)S(1)} %get-tuple-element.62), channel_id=1, source_target_pairs={{0,12},{4,0},{8,4},{12,8},{1,13},{5,1},{9,5},{13,9},{2,14},{6,2},{... | collective-permute-start | bytes 196616 | tf_op jit(solution)/shard_map/ppermute | solution.py:405
  43.5 5.7 %collective-permute-start.7 = (f32[128,128]{1,0:T(8,128)S(1)}, f32[128,128]{1,0:T(8,128)S(1)}, u32[]{:S(2)}, u32[]{:S(2)}) collective-permute-start(f32[128,128]{1,0:T(8,128)S(1)} %get-tuple-element.68.own), channel_id=1, source_target_pairs={{0,12},{4,0},{8,4},{12,8},{1,13},{5,1},{9,5},{13,9},{2,14},{6,2},{... | collective-permute-start | bytes 196616 | tf_op jit(solution)/shard_map/ppermute | solution.py:405
  46.7 5.2 %collective-permute-start.8 = (f32[128,128]{1,0:T(8,128)S(1)}, f32[128,128]{1,0:T(8,128)S(1)}, u32[]{:S(2)}, u32[]{:S(2)}) collective-permute-start(f32[128,128]{1,0:T(8,128)S(1)} %get-tuple-element.68.own), channel_id=1, source_target_pairs={{0,8},{4,12},{8,0},{12,4},{1,9},{5,13},{9,1},{13,5},{2,10},{6,14},... | collective-permute-start | bytes 196616 | tf_op jit(solution)/shard_map/ppermute | solution.py:405
  46.7 6.1 %collective-permute-start.9 = (f32[128,128]{1,0:T(8,128)S(1)}, f32[128,128]{1,0:T(8,128)S(1)}, u32[]{:S(2)}, u32[]{:S(2)}) collective-permute-start(f32[128,128]{1,0:T(8,128)S(1)} %get-tuple-element.68.own), channel_id=1, source_target_pairs={{0,4},{4,8},{8,12},{12,0},{1,5},{5,9},{9,13},{13,1},{2,6},{6,10},{... | collective-permute-start | bytes 196616 | tf_op jit(solution)/shard_map/ppermute | solution.py:405
  49.2 4.7 %collective-permute-start.10 = (f32[128,128]{1,0:T(8,128)S(1)}, f32[128,128]{1,0:T(8,128)S(1)}, u32[]{:S(2)}, u32[]{:S(2)}) collective-permute-start(f32[128,128]{1,0:T(8,128)S(1)} %collective-permute-done.7.refs_0_), channel_id=1, source_target_pairs={{0,1},{1,0},{2,3},{3,2},{4,5},{5,4},{6,7},{7,6},{8,9},{9,8},{10,11... | collective-permute-start | bytes 196616 | tf_op jit(solution)/shard_map/ppermute | solution.py:410
  51.9 2.1 %collective-permute-start.11 = (f32[128,128]{1,0:T(8,128)S(1)}, f32[128,128]{1,0:T(8,128)S(1)}, u32[]{:S(2)}, u32[]{:S(2)}) collective-permute-start(f32[128,128]{1,0:T(8,128)S(1)} %collective-permute-done.8.refs_1_), channel_id=1, source_target_pairs={{0,1},{1,0},{2,3},{3,2},{4,5},{5,4},{6,7},{7,6},{8,9},{9,8},{10,11... | collective-permute-start | bytes 196616 | tf_op jit(solution)/shard_map/ppermute | solution.py:410
  52.8 1.3 %collective-permute-start.12 = (f32[128,128]{1,0:T(8,128)S(1)}, f32[128,128]{1,0:T(8,128)S(1)}, u32[]{:S(2)}, u32[]{:S(2)}) collective-permute-start(f32[128,128]{1,0:T(8,128)S(1)} %collective-permute-done.9.refs_2_), channel_id=1, source_target_pairs={{0,1},{1,0},{2,3},{3,2},{4,5},{5,4},{6,7},{7,6},{8,9},{9,8},{10,11... | collective-permute-start | bytes 196616 | tf_op jit(solution)/shard_map/ppermute | solution.py:410
  (7 other events, 27.7 us)
